TPU v7x, 32 devices: a whole 2x2x4 slice. The times are simulated.
32 devices in a mesh: seq: 16 (over z, y, core), grp: 2 (over x).
Axes of the slice: x: 2, y: 2, z: 4, core: 2. Of those that a mesh axis runs over, the one named last changes fastest.
Arguments:
- units: bfloat16 [4096, 1024], P(('grp', 'seq')), parts along dimension 0, may hold values from -6 to 6
- durations: int32 [4096], P(('grp', 'seq')), parts along dimension 0, may hold values from 1 to 12, 12288 in all
- seg_ids: int32 [4096], P(('grp', 'seq')), parts along dimension 0, may hold values from 0 to 7, never falling along the last dimension, each value on 1 to 1024 neighbouring positions
- ln_gain: float32 [1024], replicated, may hold values from 0.1 to 1.9
- w_qkv: bfloat16 [1024, 3072], replicated, may hold values from -8 to 8
- w_out: bfloat16 [1024, 1024], replicated, may hold values from -0.1875 to 0.1875
- w_proj: bfloat16 [1024, 512], replicated, may hold values from -0.1875 to 0.1875
- conv_w: bfloat16 [5, 512, 512], replicated, may hold values from -0.125 to 0.125
- conv_b: float32 [512], replicated, may hold values from -3 to 3
- conv_gain: float32 [512], replicated, may hold values from 0.1 to 1.9
Outputs:
- frames_out: bfloat16 [24576, 512], P(('grp', 'seq')), parts along dimension 0
There are 2 independent parts, one for each index of `grp`. A program takes and returns all parts, laid end to end along the dimension named above; an argument that names none is the same for every part. Nothing has to cross between parts.
All inputs are finite; a program needn't handle non-finite values. No bound on the sum of `durations` on one device may be relied on, other than what follows from the above.
Results may differ from a plain program's by a relative error of at most 0.0098.
Values may be sent and summed in bfloat16 or wider, within the bound.
No kernel may reach another device: no remote copies, remote signals or barrier semaphores. Data moves between devices by JAX's collectives and lax.ppermute only.
A program may use at most 128 MiB of HBM per device.

v0:
```python
import functools
import math

import jax
import jax.numpy as jnp
from jax import lax
from jax.experimental import pallas as pl
from jax.experimental.pallas import tpu as pltpu
from jax.sharding import PartitionSpec as P


HEADS = 16
KERNEL = 5
SEGS = 8
DUR_MEAN = 6
EPS = 1e-05

MAIN = 128
REST = 32
WIN = MAIN + REST
GROUP = 4
STACK = GROUP * WIN
ALIGN = 8
LANES = 256
HALO = 8
LOW = -1e30
MASKED = -2e30
LOADS = 8
SMALL_VMEM = 4 << 20
EXTRA = 8
PROJECT_VMEM = 6 << 20
FRAMES_VMEM = 24 << 20


def rows_normalized(values, gain):
    mean = jnp.mean(values, axis=-1, keepdims=True)
    centred = values - mean
    variance = jnp.mean(centred * centred, axis=-1, keepdims=True)
    return centred * lax.rsqrt(variance + EPS) * gain


def pack_body(here, units, dur, seg, out, ids, sems):
    rows, width = units.shape
    count = dur.shape[1]
    copies = [
        pltpu.make_async_copy(dur, ids.at[:, pl.ds(0, count)], sems.at[0]),
        pltpu.make_async_copy(seg, ids.at[:, pl.ds(count, count)], sems.at[1]),
        pltpu.make_async_copy(units, out.at[pl.ds(0, rows)], sems.at[2]),
    ]
    for copy in copies:
        copy.start()
    out[pl.ds(rows, EXTRA), :] = jnp.zeros((EXTRA, width), jnp.bfloat16)
    copies[0].wait()
    copies[1].wait()
    line = ids[...].astype(jnp.float32).astype(jnp.bfloat16)
    out[pl.ds(rows, EXTRA), : 2 * count] = jnp.broadcast_to(line, (EXTRA, 2 * count))
    copies[2].wait()


def pack(here, units, dur, seg):
    rows, width = units.shape
    hbm = pl.BlockSpec(memory_space=pltpu.HBM)
    arrays = [pltpu.with_memory_space_constraint(array, pltpu.HBM) for array in (units, dur, seg)]
    return pl.pallas_call(
        pack_body,
        out_shape=jax.ShapeDtypeStruct((rows + EXTRA, width), units.dtype),
        in_specs=[pl.BlockSpec(memory_space=pltpu.SMEM), hbm, hbm, hbm],
        out_specs=pl.BlockSpec(memory_space=pltpu.VMEM),
        scratch_shapes=[
            pltpu.VMEM((1, 2 * dur.shape[1]), jnp.int32), pltpu.SemaphoreType.DMA((3,))
        ],
        compiler_params=pltpu.CompilerParams(vmem_limit_bytes=SMALL_VMEM),
    )(here, *arrays)


def counted(condition):
    return jnp.sum(jnp.where(condition, 1.0, 0.0)).astype(jnp.int32)


def plan(frame_count, here, meta, sc, lines, starts, ends):
    n, _, double = meta.shape
    count = double // 2
    for i in range(n):
        lines[i : i + 1, :] = meta[i].astype(jnp.float32)[:1]
    dur, seg = lines[:, :count], lines[:, count:]
    rows = lax.broadcasted_iota(jnp.int32, (count, count), 0)
    cols = lax.broadcasted_iota(jnp.int32, (count, count), 1)
    upper = jnp.where(rows <= cols, 1.0, 0.0).astype(jnp.bfloat16)
    running = jnp.dot(dur.astype(jnp.bfloat16), upper, preferred_element_type=jnp.float32)
    sums = jnp.sum(dur, axis=1, keepdims=True)
    starts[...] = jnp.zeros_like(starts)
    ends[...] = jnp.zeros_like(ends)
    before = jnp.zeros((1, 1), jnp.float32)
    for r in range(n):
        ends[r : r + 1, :] = (running[r : r + 1, :] + before).astype(jnp.int32)
        before = before + sums[r : r + 1, :]
    done = ends[pl.ds(0, n), :]
    starts[pl.ds(0, n), :] = done - dur.astype(jnp.int32)
    half = KERNEL // 2
    frame0 = here * frame_count
    first = counted(done <= jnp.maximum(frame0 - half, 0))
    last = counted(done <= jnp.minimum(frame0 + frame_count + half, n * frame_count) - 1)
    base = lax.div(first, ALIGN) * ALIGN
    windows = lax.div(last - base + WIN, WIN)
    sc[0] = jnp.minimum(base, n * count - windows * WIN)
    sc[1] = windows
    sc[2] = frame0
    for v in range(SEGS + 1):
        sc[4 + v] = counted(seg < v)


def load_body(here, source, target, token, sems):
    token[...] = jnp.zeros_like(token)
    rows = source.shape[0] // LOADS
    copies = []
    for i in range(LOADS):
        part = pl.ds(i * rows, rows)
        copies.append(pltpu.make_async_copy(source.at[part], target.at[part], sems.at[i]))
    for copy in copies:
        copy.start()
    for copy in copies:
        copy.wait()


def load(here, array):
    return pl.pallas_call(
        load_body,
        out_shape=(
            pltpu.VMEM(array.shape, array.dtype), jax.ShapeDtypeStruct((8, 128), jnp.float32)
        ),
        in_specs=[pl.BlockSpec(memory_space=pltpu.SMEM), pl.BlockSpec(memory_space=pltpu.HBM)],
        out_specs=(pl.BlockSpec(memory_space=pltpu.VMEM),) * 2,
        scratch_shapes=[pltpu.SemaphoreType.DMA((LOADS,))],
        cost_estimate=pl.CostEstimate(
            flops=0, bytes_accessed=2 * array.size * array.dtype.itemsize, transcendentals=0
        ),
        compiler_params=pltpu.CompilerParams(vmem_limit_bytes=PROJECT_VMEM),
    )(here, pltpu.with_memory_space_constraint(array, pltpu.HBM))


def project_body(step, dy, outer, here, x0, x1, gain, w, *rest):
    ks, vs, xa, meta, token, hs, sem = rest[-7:]
    rows, width = x0.shape
    rows = rows - EXTRA
    slot = lax.rem(lax.div(here[0], 4) + outer - step, outer) * 2 + (lax.rem(lax.div(here[0], 2), 2) ^ dy)
    core = lax.rem(here[0], 2)
    copies = []
    for i, ref in enumerate((x0, x1)):
        start = pl.multiple_of(slot * 2 * rows + (core ^ i) * rows, rows)
        copies.append(
            pltpu.make_async_copy(ref.at[pl.ds(0, rows)], xa.at[pl.ds(start, rows)], sem.at[i])
        )
        ids = ref.at[pl.ds(rows, EXTRA), pl.ds(0, meta.shape[2])]
        copies.append(pltpu.make_async_copy(ids, meta.at[slot * 2 + (core ^ i)], sem.at[2 + i]))
    for copy in copies:
        copy.start()
    for copy in copies:
        copy.wait()
    pair = pl.ds(pl.multiple_of(slot * 2 * rows, 2 * rows), 2 * rows)
    token[...] = jnp.zeros_like(token)
    hs[...] = rows_normalized(xa[pair, :].astype(jnp.float32), gain[...]).astype(jnp.bfloat16)
    cols = 256
    for c in range(width, 2 * width, cols):
        k = jnp.dot(hs[...], w[:, c : c + cols], preferred_element_type=jnp.float32)
        ks[slot, :, c - width : c - width + cols] = k.astype(jnp.bfloat16)
    for c in range(2 * width, 3 * width, cols):
        v = jnp.dot(hs[...], w[:, c : c + cols], preferred_element_type=jnp.float32)
        vs[slot, c - 2 * width : c - 2 * width + cols, :] = v.astype(jnp.bfloat16).T


def project(step, dy, outer, here, blocks, gain, w_qkv, previous, after, units):
    rows, width = blocks[0].shape
    rows = rows - EXTRA
    pair = 2 * rows
    pairs = units // pair
    vmem = pl.BlockSpec(memory_space=pltpu.VMEM)
    any_spec = pl.BlockSpec(memory_space=pl.ANY)
    operands = [here, *blocks, gain, w_qkv]
    in_specs = [pl.BlockSpec(memory_space=pltpu.SMEM), any_spec, any_spec, vmem, vmem]
    in_specs += [any_spec] * len(after)
    operands += list(after)
    aliases = {}
    if previous is not None:
        aliases = {len(operands) + i: i for i in range(4)}
        in_specs += [any_spec] * 4
        operands += list(previous)
    return pl.pallas_call(
        functools.partial(project_body, step, dy, outer),
        out_shape=(
            pltpu.VMEM((pairs, pair, width), jnp.bfloat16),
            pltpu.VMEM((pairs, width, pair), jnp.bfloat16),
            pltpu.VMEM((units, width), jnp.bfloat16),
            pltpu.VMEM((units // rows, EXTRA, 2 * rows), jnp.bfloat16),
            jax.ShapeDtypeStruct((8, 128), jnp.float32),
        ),
        in_specs=in_specs,
        out_specs=(vmem,) * 5,
        scratch_shapes=[pltpu.VMEM((pair, width), jnp.bfloat16), pltpu.SemaphoreType.DMA((4,))],
        input_output_aliases=aliases,
        cost_estimate=pl.CostEstimate(
            flops=2 * pair * width * 2 * width,
            bytes_accessed=2 * (width * 2 * width + 4 * pair * width),
            transcendentals=0,
        ),
        compiler_params=pltpu.CompilerParams(vmem_limit_bytes=PROJECT_VMEM),
    )(*operands)


def frames_body(
    here, meta, gain, conv_b, conv_gain, xa, keys, values, w_qkv, w_out, w_proj, conv_w,
    out, wo, wp, cw, xw, qs, begun, bias, acc, acc_rest, tops, totals, turned, red,
    expanded, sc, lines, starts, ends, sems,
):
    width = w_out.shape[0]
    channels = w_proj.shape[1]
    head = width // HEADS
    deep = GROUP * head
    frames = out.shape[0]
    tile = keys.shape[1]
    half = KERNEL // 2
    scale = math.log2(math.e) / math.sqrt(head)

    load_o = pltpu.make_async_copy(w_out, wo, sems.at[1])
    load_p = pltpu.make_async_copy(w_proj, wp, sems.at[2])
    load_c = pltpu.make_async_copy(conv_w, cw, sems.at[3])
    load_o.start()
    load_p.start()
    load_c.start()

    plan(frames, here[0], meta, sc, lines, starts, ends)
    base, windows, frame0 = sc[0], sc[1], sc[2]

    def seg_start(v):
        return sc[4 + v]

    def window(w, carry):
        r0 = pl.multiple_of(base + w * WIN, ALIGN)
        load_x = pltpu.make_async_copy(xa.at[pl.ds(r0, WIN)], xw, sems.at[4])
        load_x.start()
        lo, hi = jnp.int32(0), jnp.int32(0)
        for v in range(SEGS):
            lo = jnp.where(r0 >= seg_start(v), seg_start(v), lo)
            hi = jnp.where(r0 + WIN - 1 >= seg_start(v), seg_start(v + 1), hi)
        t0 = lax.div(lo, tile)
        t1 = lax.div(hi + tile - 1, tile)

        load_x.wait()
        h = rows_normalized(xw[...].astype(jnp.float32), gain[...]).astype(jnp.bfloat16)
        q = jnp.dot(h, w_qkv[:, :width], preferred_element_type=jnp.float32).astype(jnp.bfloat16)
        owner = lax.broadcasted_iota(jnp.int32, (WIN, deep), 1) // head
        zero = jnp.zeros((WIN, deep), jnp.bfloat16)
        for g in range(HEADS // GROUP):
            part = q[:, g * deep : (g + 1) * deep]
            for j in range(GROUP):
                alone = jnp.where(owner == j, part, zero)
                qs[g, j * MAIN : (j + 1) * MAIN, :] = alone[:MAIN]
                start = GROUP * MAIN + j * REST
                qs[g, start : start + REST, :] = alone[MAIN:]
        acc[...] = jnp.zeros_like(acc)
        acc_rest[...] = jnp.zeros_like(acc_rest)
        tops[...] = jnp.full_like(tops, LOW)
        totals[...] = jnp.zeros_like(totals)

        lane = lax.broadcasted_iota(jnp.int32, (1, 2 * MAIN), 1)
        row = r0 + jnp.where(lane < MAIN, lane, MAIN + (lane - MAIN) % REST)
        row_lo = jnp.zeros_like(row)
        row_hi = jnp.zeros_like(row)
        for v in range(SEGS):
            row_lo = jnp.where(row >= seg_start(v), seg_start(v), row_lo)
            row_hi = jnp.where(row >= seg_start(v), seg_start(v + 1), row_hi)

        def scores(t, g):
            dims = slice(g * deep, (g + 1) * deep)
            return lax.dot_general(
                keys[t, :, dims], qs[g], (((1,), (1,)), ((), ())),
                preferred_element_type=jnp.float32,
            )

        begun[...] = scores(t0, 0)

        def key_step(t, c):
            key = t * tile + lax.broadcasted_iota(jnp.int32, (tile, 2 * MAIN), 0)
            bias[...] = jnp.where((key >= row_lo) & (key < row_hi), 0.0, MASKED)
            main = bias[:, :MAIN]
            mask = jnp.concatenate([main] * GROUP + [bias[:, MAIN:]], axis=1)
            groups = HEADS // GROUP

            ahead = begun[...]
            for g in range(groups):
                dims = slice(g * deep, (g + 1) * deep)
                s = ahead * scale + mask
                if g + 1 < groups:
                    ahead = scores(t, g + 1)
                else:
                    begun[...] = scores(jnp.minimum(t + 1, t1 - 1), 0)
                top = tops[g]
                new_top = jnp.maximum(top, jnp.max(s, axis=0, keepdims=True))
                expo = jnp.exp2(s - new_top)
                alpha = jnp.exp2(top - new_top)
                tops[g] = new_top
                totals[g] = totals[g] * alpha + jnp.sum(expo, axis=0, keepdims=True)
                expo = expo.astype(jnp.bfloat16)
                for j in range(GROUP):
                    lanes = slice(j * MAIN, (j + 1) * MAIN)
                    start = g * deep + j * head
                    acc[g, j] = acc[g, j] * alpha[:, lanes] + jnp.dot(
                        values[t, start : start + head, :], expo[:, lanes],
                        preferred_element_type=jnp.float32,
                    )
                acc_rest[g] = acc_rest[g] * alpha[:, GROUP * MAIN :] + jnp.dot(
                    values[t, dims, :], expo[:, GROUP * MAIN :],
                    preferred_element_type=jnp.float32,
                )
            return c

        lax.fori_loop(t0, t1, key_step, 0)

        for g in range(HEADS // GROUP):
            total = totals[g]
            total = jnp.where(total == 0.0, 1.0, total)
            for j in range(GROUP):
                start = g * deep + j * head
                lanes = slice(j * MAIN, (j + 1) * MAIN)
                turned[start : start + head, :MAIN] = acc[g, j] / total[:, lanes]
            rest = acc_rest[g] / total[:, GROUP * MAIN :]
            for j in range(GROUP):
                start = g * deep + j * head
                turned[start : start + head, MAIN:WIN] = rest[
                    j * head : (j + 1) * head, j * REST : (j + 1) * REST
                ]
        attended = turned[...].T[:WIN].astype(jnp.bfloat16)

        @pl.when(w == 0)
        def _():
            load_o.wait()
            load_p.wait()

        mixed = jnp.dot(attended, wo[...], preferred_element_type=jnp.float32) + xw[...].astype(
            jnp.float32
        )
        reduced = jnp.dot(
            mixed.astype(jnp.bfloat16), wp[...], preferred_element_type=jnp.float32
        ).astype(jnp.bfloat16)
        red[pl.ds(0, WIN), :] = reduced
        red[pl.ds(WIN, LANES - WIN), :] = jnp.zeros((LANES - WIN, channels), jnp.bfloat16)
        shape = (frames + 2 * HALO, LANES)
        frame = frame0 - HALO + lax.broadcasted_iota(jnp.int32, shape, 0)
        lanes = starts.shape[1]
        row0 = lax.div(r0, lanes)
        shift = 3 * lanes - lax.rem(r0, lanes)

        def cut(ref):
            line = jnp.concatenate([ref[pl.ds(row0 + i, 1), :] for i in range(3)], axis=1)
            line = pltpu.roll(jnp.broadcast_to(line, (8, 3 * lanes)), shift, 1)[:1, :LANES]
            return jnp.where(lax.broadcasted_iota(jnp.int32, (1, LANES), 1) < WIN, line, 0)

        pick = jnp.where((frame >= cut(starts)) & (frame < cut(ends)), 1.0, 0.0).astype(jnp.bfloat16)
        rows = jnp.dot(pick, red[...], preferred_element_type=jnp.float32)

        @pl.when(w == 0)
        def _():
            expanded[...] = rows

        @pl.when(w > 0)
        def _():
            expanded[...] += rows

        return carry

    lax.fori_loop(0, windows, window, 0)

    load_c.wait()
    block = 256
    for b in range(frames // block):
        conv = jnp.zeros((block, channels), jnp.float32) + conv_b[...]
        for tap in range(KERNEL):
            part = expanded[pl.ds(b * block + HALO - half + tap, block), :].astype(jnp.bfloat16)
            conv = conv + jnp.dot(part, cw[tap], preferred_element_type=jnp.float32)
        result = expanded[pl.ds(b * block + HALO, block), :] + rows_normalized(
            jnp.maximum(conv, 0.0), conv_gain[...]
        )
        out[pl.ds(b * block, block), :] = result.astype(jnp.bfloat16)


def frames_call(here, meta, gain, conv_b, conv_gain, xa, ks, vs, w_qkv, w_out, w_proj, conv_w, frames):
    _, width = xa.shape
    channels = w_proj.shape[1]
    head = width // HEADS
    hbm = pl.BlockSpec(memory_space=pltpu.HBM)
    vmem = pl.BlockSpec(memory_space=pltpu.VMEM)
    groups = HEADS // GROUP
    return pl.pallas_call(
        frames_body,
        out_shape=jax.ShapeDtypeStruct((frames, channels), jnp.bfloat16),
        in_specs=[pl.BlockSpec(memory_space=pltpu.SMEM)] + [vmem] * 8 + [hbm] * 3,
        out_specs=vmem,
        scratch_shapes=[
            pltpu.VMEM((width, width), jnp.bfloat16),
            pltpu.VMEM((width, channels), jnp.bfloat16),
            pltpu.VMEM((KERNEL, channels, channels), jnp.bfloat16),
            pltpu.VMEM((WIN, width), jnp.bfloat16),
            pltpu.VMEM((groups, STACK, GROUP * head), jnp.bfloat16),
            pltpu.VMEM((ks.shape[1], STACK), jnp.float32),
            pltpu.VMEM((ks.shape[1], 2 * MAIN), jnp.float32),
            pltpu.VMEM((groups, GROUP, head, MAIN), jnp.float32),
            pltpu.VMEM((groups, GROUP * head, GROUP * REST), jnp.float32),
            pltpu.VMEM((groups, 1, STACK), jnp.float32),
            pltpu.VMEM((groups, 1, STACK), jnp.float32),
            pltpu.VMEM((width, 2 * MAIN), jnp.float32),
            pltpu.VMEM((LANES, channels), jnp.bfloat16),
            pltpu.VMEM((frames + 2 * HALO, channels), jnp.float32),
            pltpu.SMEM((SEGS + 5,), jnp.int32),
            pltpu.VMEM((meta.shape[0], meta.shape[2]), jnp.float32),
            pltpu.VMEM((meta.shape[0] + 8, meta.shape[2] // 2), jnp.int32),
            pltpu.VMEM((meta.shape[0] + 8, meta.shape[2] // 2), jnp.int32),
            pltpu.SemaphoreType.DMA((5,)),
        ],
        compiler_params=pltpu.CompilerParams(vmem_limit_bytes=FRAMES_VMEM),
    )(here, meta, gain, conv_b, conv_gain, xa, ks, vs, w_qkv, w_out, w_proj, conv_w)


def local(units, durations, seg_ids, ln_gain, w_qkv, w_out, w_proj, conv_w, conv_b, conv_gain):
    n = lax.axis_size("seq")
    outer = n // 4
    here = lax.axis_index("seq")
    count = units.shape[0]
    total = n * count
    frame_count = DUR_MEAN * count

    def place(z, y, c):
        return (z * 2 + y) * 2 + c

    def pairs(step, dy, dc):
        return [
            (place(z, y, c), place((z + step) % outer, y ^ dy, c ^ dc))
            for z in range(outer)
            for y in range(2)
            for c in range(2)
        ]

    def send(value, step, dy=0, dc=0):
        return lax.ppermute(value, "seq", pairs(step, dy, dc))

    gain = ln_gain[None, :]
    w_out, w_proj, conv_w = [
        pltpu.with_memory_space_constraint(w, pltpu.HBM) for w in (w_out, w_proj, conv_w)
    ]
    where = here.reshape(1)

    def kernel(distance, dy, blocks, state, *after):
        *state, token = project(
            distance % outer, dy, outer, where, blocks, gain, w_qkv, state, after, total
        )
        return state, token

    w_qkv, token = load(where, w_qkv)
    state = None
    far_up, far_down = outer // 2, (outer - 1) // 2
    up = down = own = pack(where, units, durations[None, :], seg_ids[None, :])
    arrived = [(0, own)]
    waiting = []
    for step in range(far_up + 1):
        following = []
        if step < far_up:
            up = send(up, 1)
            following.append((step + 1, up))
        if step < far_down:
            down = send(down, outer - 1)
            following.append((-(step + 1), down))
        for pair in waiting:
            state, token = kernel(*pair, state, token)
        if waiting and following:
            held = lax.optimization_barrier((token, *[block for _, block in arrived]))
            token = held[0]
            arrived = [(d, block) for (d, _), block in zip(arrived, held[1:])]
        sides = []
        for d, block in arrived:
            if step == far_up and step > 1:
                across = send(waiting_up, 1)
            else:
                across = send(block, 0, 1, 0)
            sides.append((d, block, across, send(block, 0, 0, 1)))
        for d, block, across, beside in sides:
            state, token = kernel(d, 0, (block, beside), state, token)
        if step == 0:
            ((d, _, across, _),) = sides
            token, across = lax.optimization_barrier((token, across))
            diagonal = send(across, 0, 0, 1)
            state, token = kernel(d, 1, (across, diagonal), state, token)
        halves = [across for _, _, across, _ in sides]
        if following:
            held = lax.optimization_barrier((token, *[block for _, block in following]))
            token = held[0]
            following = [(d, block) for (d, _), block in zip(following, held[1:])]
            up = following[0][1]
            down = following[1][1] if len(following) > 1 else None
        waiting = []
        for (d, _, _, _), across in zip(sides if step > 0 else (), halves):
            token, across = lax.optimization_barrier((token, across))
            waiting.append((d, 1, (across, send(across, 0, 0, 1))))
        waiting_up = sides[0][2]
        arrived = following
    for pair in waiting:
        state, token = kernel(*pair, state, token)

    ks, vs, xa, meta = state
    return frames_call(
        where, meta, gain, conv_b[None, :], conv_gain[None, :], xa, ks, vs, w_qkv, w_out, w_proj,
        conv_w, frame_count,
    )


def solution(mesh):
    split = P(("grp", "seq"))
    in_specs = (P(("grp", "seq"), None), split, split) + (P(),) * 7
    return jax.shard_map(
        local, mesh=mesh, in_specs=in_specs, out_specs=P(("grp", "seq"), None), check_vma=False
    )
```

profile of v0, /device:TPU:0, one launch (start us, length us, event | category | flops | bytes accessed | tf_op | source)
XLA Modules:
  0.0 70.3 jit_solution(4644464006458208498)
XLA Ops:
  0.0 0.0 copy-start
  0.0 1.0 %shard_map.100.x0 = bf16[136,1024]{1,0:T(8,128)(2,1)S(1)} custom-call(s32[1]{0:T(128)} %bitcast.here, bf16[128,1024]{1,0:T(8,128)(2,1)} %units.1, s32[1,128]{1,0:T(1,128)} %bitcast.17, s32[1,128]{1,0:T(1,128)} %bitcast.18), custom_call_target="tpu_custom_call" | custom-call | tf_op jit(solution)/shard_map/pallas_call | solution.py:64
  1.0 0.6 collective-permute-start
  1.6 2.6 %collective-permute-start.1 = (bf16[136,1024]{1,0:T(8,128)(2,1)S(1)}, bf16[136,1024]{1,0:T(8,128)(2,1)S(1)}, u32[]{:S(2)}, u32[]{:S(2)}) collective-permute-start(bf16[136,1024]{1,0:T(8,128)(2,1)S(1)} %shard_map.100.x0), channel_id=1, source_target_pairs={{0,4},{2,6},{4,0},{6,2},{8,12},{10,14},{12,8},{14,10},{16,20},{18,... | collective-permute-start | bytes 835592 | tf_op jit(solution)/shard_map/ppermute | solution.py:442
  4.2 2.9 %shard_map.101 = (bf16[1024,3072]{1,0:T(8,128)(2,1)S(1)}, f32[8,128]{1,0:T(8,128)S(1)}) custom-call(s32[1]{0:T(128)} %bitcast.here, bf16[1024,3072]{1,0:T(8,128)(2,1)} %source.1), custom_call_target="tpu_custom_call" | custom-call | bytes 12582912 | tf_op jit(solution)/shard_map/pallas_call | solution.py:126
  7.0 0.0 collective-permute-done.x1
  7.0 0.0 copy-done
  7.1 1.7 %shard_map.102 = (bf16[8,256,1024]{2,1,0:T(8,128)(2,1)S(1)}, bf16[8,1024,256]{2,1,0:T(8,128)(2,1)S(1)}, bf16[2048,1024]{1,0:T(8,128)(2,1)S(1)}, bf16[16,8,256]{2,1,0:T(8,128)(2,1)S(1)}, f32[8,128]{1,0:T(8,128)S(1)}) custom-call(s32[1]{0:T(128)} %bitcast.here, bf16[136,1024]{1,0:T(8,128)(2,1)S(1)} %shard_map.100.x0, ...), custom_call_target="tpu_custom_call" | custom-call | flops 1073741824 | bytes 6291456 | tf_op jit(solution)/shard_map/pallas_call | solution.py:187
  8.8 2.6 %collective-permute-done.1.x0 = bf16[136,1024]{1,0:T(8,128)(2,1)S(1)} collective-permute-done((bf16[136,1024]{1,0:T(8,128)(2,1)S(1)}, bf16[136,1024]{1,0:T(8,128)(2,1)S(1)}, u32[]{:S(2)}, u32[]{:S(2)}) %collective-permute-start.1) | collective-permute-done | bytes 278560 | tf_op jit(solution)/shard_map/ppermute | solution.py:442
  11.4 0.0 collective-permute-start.2
  11.4 1.8 %collective-permute-start.3 = (bf16[136,1024]{1,0:T(8,128)(2,1)S(1)}, bf16[136,1024]{1,0:T(8,128)(2,1)S(1)}, u32[]{:S(2)}, u32[]{:S(2)}) collective-permute-start(bf16[136,1024]{1,0:T(8,128)(2,1)S(1)} %shard_map.100.x0), channel_id=1, source_target_pairs={{0,8},{2,10},{4,12},{6,14},{8,16},{10,18},{12,20},{14,22},{16,24},... | collective-permute-start | bytes 835592 | tf_op jit(solution)/shard_map/ppermute | solution.py:442
  13.2 2.0 %collective-permute-start.4 = (bf16[136,1024]{1,0:T(8,128)(2,1)S(1)}, bf16[136,1024]{1,0:T(8,128)(2,1)S(1)}, u32[]{:S(2)}, u32[]{:S(2)}) collective-permute-start(bf16[136,1024]{1,0:T(8,128)(2,1)S(1)} %shard_map.100.x0), channel_id=1, source_target_pairs={{0,24},{2,26},{4,28},{6,30},{8,0},{10,2},{12,4},{14,6},{16,8},{18,... | collective-permute-start | bytes 835592 | tf_op jit(solution)/shard_map/ppermute | solution.py:442
  15.3 0.0 collective-permute-done.2.x1
  15.3 1.7 %shard_map.103 = (bf16[8,256,1024]{2,1,0:T(8,128)(2,1)S(1)}, bf16[8,1024,256]{2,1,0:T(8,128)(2,1)S(1)}, bf16[2048,1024]{1,0:T(8,128)(2,1)S(1)}, bf16[16,8,256]{2,1,0:T(8,128)(2,1)S(1)}, f32[8,128]{1,0:T(8,128)S(1)}) custom-call(s32[1]{0:T(128)} %bitcast.here, ...), custom_call_target="tpu_custom_call", output_to_operand_aliasing={{0}: (6, {}), {1}: (7, {}), {2}: (8, {}), {3}: (9, {})} | custom-call | flops 1073741824 | bytes 6291456 | tf_op jit(solution)/shard_map/pallas_call | solution.py:187
  17.0 5.8 %collective-permute-done.3.x0 = bf16[136,1024]{1,0:T(8,128)(2,1)S(1)} collective-permute-done((bf16[136,1024]{1,0:T(8,128)(2,1)S(1)}, bf16[136,1024]{1,0:T(8,128)(2,1)S(1)}, u32[]{:S(2)}, u32[]{:S(2)}) %collective-permute-start.3) | collective-permute-done | bytes 278560 | tf_op jit(solution)/shard_map/ppermute | solution.py:442
  22.8 5.2 %collective-permute-done.4.x0 = bf16[136,1024]{1,0:T(8,128)(2,1)S(1)} collective-permute-done((bf16[136,1024]{1,0:T(8,128)(2,1)S(1)}, bf16[136,1024]{1,0:T(8,128)(2,1)S(1)}, u32[]{:S(2)}, u32[]{:S(2)}) %collective-permute-start.4) | collective-permute-done | bytes 278560 | tf_op jit(solution)/shard_map/ppermute | solution.py:442
  28.0 0.0 collective-permute-start.6
  28.0 0.5 collective-permute-start.5
  28.5 1.1 %collective-permute-start.7 = (bf16[136,1024]{1,0:T(8,128)(2,1)S(1)}, bf16[136,1024]{1,0:T(8,128)(2,1)S(1)}, u32[]{:S(2)}, u32[]{:S(2)}) collective-permute-start(bf16[136,1024]{1,0:T(8,128)(2,1)S(1)} %collective-permute-done.3.x0), channel_id=1, source_target_pairs={{0,8},{2,10},{4,12},{6,14},{8,16},{10,18},{12,20},{14,22},{16,24},... | collective-permute-start | bytes 835592 | tf_op jit(solution)/shard_map/ppermute | solution.py:442
  29.6 1.5 %collective-permute-start.9 = (bf16[136,1024]{1,0:T(8,128)(2,1)S(1)}, bf16[136,1024]{1,0:T(8,128)(2,1)S(1)}, u32[]{:S(2)}, u32[]{:S(2)}) collective-permute-start(bf16[136,1024]{1,0:T(8,128)(2,1)S(1)} %collective-permute-done.3.x0), channel_id=1, source_target_pairs={{0,4},{2,6},{4,0},{6,2},{8,12},{10,14},{12,8},{14,10},{16,20},{18,... | collective-permute-start | bytes 835592 | tf_op jit(solution)/shard_map/ppermute | solution.py:442
  31.1 0.5 collective-permute-start.10
  31.6 0.0 collective-permute-done.6.x1
  31.7 1.7 %shard_map.104 = (bf16[8,256,1024]{2,1,0:T(8,128)(2,1)S(1)}, bf16[8,1024,256]{2,1,0:T(8,128)(2,1)S(1)}, bf16[2048,1024]{1,0:T(8,128)(2,1)S(1)}, bf16[16,8,256]{2,1,0:T(8,128)(2,1)S(1)}, f32[8,128]{1,0:T(8,128)S(1)}) custom-call(s32[1]{0:T(128)} %bitcast.here, ...), custom_call_target="tpu_custom_call", output_to_operand_aliasing={{0}: (6, {}), {1}: (7, {}), {2}: (8, {}), {3}: (9, {})} | custom-call | flops 1073741824 | bytes 6291456 | tf_op jit(solution)/shard_map/pallas_call | solution.py:187
  33.4 0.0 collective-permute-done.5.x1
  33.4 1.7 %shard_map.105 = (bf16[8,256,1024]{2,1,0:T(8,128)(2,1)S(1)}, bf16[8,1024,256]{2,1,0:T(8,128)(2,1)S(1)}, bf16[2048,1024]{1,0:T(8,128)(2,1)S(1)}, bf16[16,8,256]{2,1,0:T(8,128)(2,1)S(1)}, f32[8,128]{1,0:T(8,128)S(1)}) custom-call(s32[1]{0:T(128)} %bitcast.here, ...), custom_call_target="tpu_custom_call", output_to_operand_aliasing={{0}: (6, {}), {1}: (7, {}), {2}: (8, {}), {3}: (9, {})} | custom-call | flops 1073741824 | bytes 6291456 | tf_op jit(solution)/shard_map/pallas_call | solution.py:187
  35.1 3.8 %collective-permute-done.7.x0 = bf16[136,1024]{1,0:T(8,128)(2,1)S(1)} collective-permute-done((bf16[136,1024]{1,0:T(8,128)(2,1)S(1)}, bf16[136,1024]{1,0:T(8,128)(2,1)S(1)}, u32[]{:S(2)}, u32[]{:S(2)}) %collective-permute-start.7) | collective-permute-done | bytes 278560 | tf_op jit(solution)/shard_map/ppermute | solution.py:442
  38.9 0.3 collective-permute-done.9.x0
  39.1 0.0 collective-permute-start.12
  39.2 4.8 %collective-permute-done.10.x0 = bf16[136,1024]{1,0:T(8,128)(2,1)S(1)} collective-permute-done((bf16[136,1024]{1,0:T(8,128)(2,1)S(1)}, bf16[136,1024]{1,0:T(8,128)(2,1)S(1)}, u32[]{:S(2)}, u32[]{:S(2)}) %collective-permute-start.10) | collective-permute-done | bytes 278560 | tf_op jit(solution)/shard_map/ppermute | solution.py:442
  43.9 0.0 collective-permute-start.11
  43.9 0.5 collective-permute-start.8
  44.4 0.7 collective-permute-start.13
  45.1 0.0 collective-permute-done.12.x1
  45.1 1.7 %shard_map.106 = (bf16[8,256,1024]{2,1,0:T(8,128)(2,1)S(1)}, bf16[8,1024,256]{2,1,0:T(8,128)(2,1)S(1)}, bf16[2048,1024]{1,0:T(8,128)(2,1)S(1)}, bf16[16,8,256]{2,1,0:T(8,128)(2,1)S(1)}, f32[8,128]{1,0:T(8,128)S(1)}) custom-call(s32[1]{0:T(128)} %bitcast.here, ...), custom_call_target="tpu_custom_call", output_to_operand_aliasing={{0}: (6, {}), {1}: (7, {}), {2}: (8, {}), {3}: (9, {})} | custom-call | flops 1073741824 | bytes 6291456 | tf_op jit(solution)/shard_map/pallas_call | solution.py:187
  46.8 0.0 collective-permute-done.11.x1
  46.8 1.7 %shard_map.107 = (bf16[8,256,1024]{2,1,0:T(8,128)(2,1)S(1)}, bf16[8,1024,256]{2,1,0:T(8,128)(2,1)S(1)}, bf16[2048,1024]{1,0:T(8,128)(2,1)S(1)}, bf16[16,8,256]{2,1,0:T(8,128)(2,1)S(1)}, f32[8,128]{1,0:T(8,128)S(1)}) custom-call(s32[1]{0:T(128)} %bitcast.here, ...), custom_call_target="tpu_custom_call", output_to_operand_aliasing={{0}: (6, {}), {1}: (7, {}), {2}: (8, {}), {3}: (9, {})} | custom-call | flops 1073741824 | bytes 6291456 | tf_op jit(solution)/shard_map/pallas_call | solution.py:187
  48.6 0.0 collective-permute-done.8.x1
  48.6 1.7 %shard_map.108 = (bf16[8,256,1024]{2,1,0:T(8,128)(2,1)S(1)}, bf16[8,1024,256]{2,1,0:T(8,128)(2,1)S(1)}, bf16[2048,1024]{1,0:T(8,128)(2,1)S(1)}, bf16[16,8,256]{2,1,0:T(8,128)(2,1)S(1)}, f32[8,128]{1,0:T(8,128)S(1)}) custom-call(s32[1]{0:T(128)} %bitcast.here, ...), custom_call_target="tpu_custom_call", output_to_operand_aliasing={{0}: (6, {}), {1}: (7, {}), {2}: (8, {}), {3}: (9, {})} | custom-call | flops 1073741824 | bytes 6291456 | tf_op jit(solution)/shard_map/pallas_call | solution.py:187
  50.3 4.5 %collective-permute-done.13.x0 = bf16[136,1024]{1,0:T(8,128)(2,1)S(1)} collective-permute-done((bf16[136,1024]{1,0:T(8,128)(2,1)S(1)}, bf16[136,1024]{1,0:T(8,128)(2,1)S(1)}, u32[]{:S(2)}, u32[]{:S(2)}) %collective-permute-start.13) | collective-permute-done | bytes 278560 | tf_op jit(solution)/shard_map/ppermute | solution.py:442
  54.8 0.0 collective-permute-start.14
  54.8 1.6 %collective-permute-done.14.x1 = bf16[136,1024]{1,0:T(8,128)(2,1)S(1)} collective-permute-done((bf16[136,1024]{1,0:T(8,128)(2,1)S(1)}, bf16[136,1024]{1,0:T(8,128)(2,1)S(1)}, u32[]{:S(2)}, u32[]{:S(2)}) %collective-permute-start.14) | collective-permute-done | bytes 278560 | tf_op jit(solution)/shard_map/ppermute | solution.py:442
  56.4 0.0 copy-start.1
  56.4 0.0 copy-start.2
  56.4 2.2 %shard_map.109 = (bf16[8,256,1024]{2,1,0:T(8,128)(2,1)S(1)}, bf16[8,1024,256]{2,1,0:T(8,128)(2,1)S(1)}, bf16[2048,1024]{1,0:T(8,128)(2,1)S(1)}, bf16[16,8,256]{2,1,0:T(8,128)(2,1)S(1)}, f32[8,128]{1,0:T(8,128)}) custom-call(s32[1]{0:T(128)} %bitcast.here, ...), custom_call_target="tpu_custom_call", output_to_operand_aliasing={{0}: (6, {}), {1}: (7, {}), {2}: (8, {}), {3}: (9, {})} | custom-call | flops 1073741824 | bytes 6291456 | tf_op jit(solution)/shard_map/pallas_call | solution.py:187
  58.6 0.0 copy-done.1
  58.6 0.0 copy-done.2
  58.6 11.5 %shard_map.110 = bf16[768,512]{1,0:T(8,128)(2,1)} custom-call(s32[1]{0:T(128)} %bitcast.here, bf16[16,8,256]{2,1,0:T(8,128)(2,1)S(1)} %get-tuple-element.109.meta, f32[1,1024]{1,0:T(1,128)S(1)} %bitcast.14, f32[1,512]{1,0:T(1,128)S(1)} %bitcast.15, f32[1,512]{1,0:T(1,128)S(1)} %bitcast.16, bf16[2048,1024]{1,0:T(8,128)(2,1)S(1)} %get-tuple-element.110.xa, ...), custom_call_target="tpu_custom_call" | custom-call | tf_op jit(solution)/shard_map/pallas_call | solution.py:392
Async XLA Ops:
  0.0 7.0 %copy-start = (f32[1024]{0:T(1024)S(1)}, f32[1024]{0:T(1024)}, u32[]{:S(2)}) copy-start(f32[1024]{0:T(1024)} %param.13) | copy-start | bytes 12292
  1.0 6.0 %collective-permute-start = (bf16[136,1024]{1,0:T(8,128)(2,1)S(1)}, bf16[136,1024]{1,0:T(8,128)(2,1)S(1)}, u32[]{:S(2)}, u32[]{:S(2)}) collective-permute-start(bf16[136,1024]{1,0:T(8,128)(2,1)S(1)} %shard_map.100.x0), channel_id=1, source_target_pairs={{0,2},{2,0},{4,6},{6,4},{8,10},{10,8},{12,14},{14,12},{16,18},{18,... | collective-permute-start | bytes 835592 | tf_op jit(solution)/shard_map/ppermute | solution.py:442
  1.6 9.8 %collective-permute-start.1 = (bf16[136,1024]{1,0:T(8,128)(2,1)S(1)}, bf16[136,1024]{1,0:T(8,128)(2,1)S(1)}, u32[]{:S(2)}, u32[]{:S(2)}) collective-permute-start(bf16[136,1024]{1,0:T(8,128)(2,1)S(1)} %shard_map.100.x0), channel_id=1, source_target_pairs={{0,4},{2,6},{4,0},{6,2},{8,12},{10,14},{12,8},{14,10},{16,20},{18,... | collective-permute-start | bytes 835592 | tf_op jit(solution)/shard_map/ppermute | solution.py:442
  11.4 3.8 %collective-permute-start.2 = (bf16[136,1024]{1,0:T(8,128)(2,1)S(1)}, bf16[136,1024]{1,0:T(8,128)(2,1)S(1)}, u32[]{:S(2)}, u32[]{:S(2)}) collective-permute-start(bf16[136,1024]{1,0:T(8,128)(2,1)S(1)} %collective-permute-done.1.x0), channel_id=1, source_target_pairs={{0,2},{2,0},{4,6},{6,4},{8,10},{10,8},{12,14},{14,12},{16,18},{18,... | collective-permute-start | bytes 835592 | tf_op jit(solution)/shard_map/ppermute | solution.py:442
  11.4 11.4 %collective-permute-start.3 = (bf16[136,1024]{1,0:T(8,128)(2,1)S(1)}, bf16[136,1024]{1,0:T(8,128)(2,1)S(1)}, u32[]{:S(2)}, u32[]{:S(2)}) collective-permute-start(bf16[136,1024]{1,0:T(8,128)(2,1)S(1)} %shard_map.100.x0), channel_id=1, source_target_pairs={{0,8},{2,10},{4,12},{6,14},{8,16},{10,18},{12,20},{14,22},{16,24},... | collective-permute-start | bytes 835592 | tf_op jit(solution)/shard_map/ppermute | solution.py:442
  13.2 14.8 %collective-permute-start.4 = (bf16[136,1024]{1,0:T(8,128)(2,1)S(1)}, bf16[136,1024]{1,0:T(8,128)(2,1)S(1)}, u32[]{:S(2)}, u32[]{:S(2)}) collective-permute-start(bf16[136,1024]{1,0:T(8,128)(2,1)S(1)} %shard_map.100.x0), channel_id=1, source_target_pairs={{0,24},{2,26},{4,28},{6,30},{8,0},{10,2},{12,4},{14,6},{16,8},{18,... | collective-permute-start | bytes 835592 | tf_op jit(solution)/shard_map/ppermute | solution.py:442
  28.0 3.7 %collective-permute-start.6 = (bf16[136,1024]{1,0:T(8,128)(2,1)S(1)}, bf16[136,1024]{1,0:T(8,128)(2,1)S(1)}, u32[]{:S(2)}, u32[]{:S(2)}) collective-permute-start(bf16[136,1024]{1,0:T(8,128)(2,1)S(1)} %collective-permute-done.3.x0), channel_id=1, source_target_pairs={{0,2},{2,0},{4,6},{6,4},{8,10},{10,8},{12,14},{14,12},{16,18},{18,... | collective-permute-start | bytes 835592 | tf_op jit(solution)/shard_map/ppermute | solution.py:442
  28.0 5.4 %collective-permute-start.5 = (bf16[136,1024]{1,0:T(8,128)(2,1)S(1)}, bf16[136,1024]{1,0:T(8,128)(2,1)S(1)}, u32[]{:S(2)}, u32[]{:S(2)}) collective-permute-start(bf16[136,1024]{1,0:T(8,128)(2,1)S(1)} %collective-permute-done.4.x0), channel_id=1, source_target_pairs={{0,2},{2,0},{4,6},{6,4},{8,10},{10,8},{12,14},{14,12},{16,18},{18,... | collective-permute-start | bytes 835592 | tf_op jit(solution)/shard_map/ppermute | solution.py:442
  28.5 10.4 %collective-permute-start.7 = (bf16[136,1024]{1,0:T(8,128)(2,1)S(1)}, bf16[136,1024]{1,0:T(8,128)(2,1)S(1)}, u32[]{:S(2)}, u32[]{:S(2)}) collective-permute-start(bf16[136,1024]{1,0:T(8,128)(2,1)S(1)} %collective-permute-done.3.x0), channel_id=1, source_target_pairs={{0,8},{2,10},{4,12},{6,14},{8,16},{10,18},{12,20},{14,22},{16,24},... | collective-permute-start | bytes 835592 | tf_op jit(solution)/shard_map/ppermute | solution.py:442
  29.6 9.5 %collective-permute-start.9 = (bf16[136,1024]{1,0:T(8,128)(2,1)S(1)}, bf16[136,1024]{1,0:T(8,128)(2,1)S(1)}, u32[]{:S(2)}, u32[]{:S(2)}) collective-permute-start(bf16[136,1024]{1,0:T(8,128)(2,1)S(1)} %collective-permute-done.3.x0), channel_id=1, source_target_pairs={{0,4},{2,6},{4,0},{6,2},{8,12},{10,14},{12,8},{14,10},{16,20},{18,... | collective-permute-start | bytes 835592 | tf_op jit(solution)/shard_map/ppermute | solution.py:442
  31.1 12.8 %collective-permute-start.10 = (bf16[136,1024]{1,0:T(8,128)(2,1)S(1)}, bf16[136,1024]{1,0:T(8,128)(2,1)S(1)}, u32[]{:S(2)}, u32[]{:S(2)}) collective-permute-start(bf16[136,1024]{1,0:T(8,128)(2,1)S(1)} %collective-permute-done.4.x0), channel_id=1, source_target_pairs={{0,4},{2,6},{4,0},{6,2},{8,12},{10,14},{12,8},{14,10},{16,20},{18,... | collective-permute-start | bytes 835592 | tf_op jit(solution)/shard_map/ppermute | solution.py:442
  39.1 6.0 %collective-permute-start.12 = (bf16[136,1024]{1,0:T(8,128)(2,1)S(1)}, bf16[136,1024]{1,0:T(8,128)(2,1)S(1)}, u32[]{:S(2)}, u32[]{:S(2)}) collective-permute-start(bf16[136,1024]{1,0:T(8,128)(2,1)S(1)} %collective-permute-done.9.x0), channel_id=1, source_target_pairs={{0,2},{2,0},{4,6},{6,4},{8,10},{10,8},{12,14},{14,12},{16,18},{18,... | collective-permute-start | bytes 835592 | tf_op jit(solution)/shard_map/ppermute | solution.py:442
  43.9 2.9 %collective-permute-start.11 = (bf16[136,1024]{1,0:T(8,128)(2,1)S(1)}, bf16[136,1024]{1,0:T(8,128)(2,1)S(1)}, u32[]{:S(2)}, u32[]{:S(2)}) collective-permute-start(bf16[136,1024]{1,0:T(8,128)(2,1)S(1)} %collective-permute-done.10.x0), channel_id=1, source_target_pairs={{0,2},{2,0},{4,6},{6,4},{8,10},{10,8},{12,14},{14,12},{16,18},{18,... | collective-permute-start | bytes 835592 | tf_op jit(solution)/shard_map/ppermute | solution.py:442
  43.9 4.7 %collective-permute-start.8 = (bf16[136,1024]{1,0:T(8,128)(2,1)S(1)}, bf16[136,1024]{1,0:T(8,128)(2,1)S(1)}, u32[]{:S(2)}, u32[]{:S(2)}) collective-permute-start(bf16[136,1024]{1,0:T(8,128)(2,1)S(1)} %collective-permute-done.7.x0), channel_id=1, source_target_pairs={{0,2},{2,0},{4,6},{6,4},{8,10},{10,8},{12,14},{14,12},{16,18},{18,... | collective-permute-start | bytes 835592 | tf_op jit(solution)/shard_map/ppermute | solution.py:442
  44.4 10.4 %collective-permute-start.13 = (bf16[136,1024]{1,0:T(8,128)(2,1)S(1)}, bf16[136,1024]{1,0:T(8,128)(2,1)S(1)}, u32[]{:S(2)}, u32[]{:S(2)}) collective-permute-start(bf16[136,1024]{1,0:T(8,128)(2,1)S(1)} %collective-permute-done.9.x0), channel_id=1, source_target_pairs={{0,8},{2,10},{4,12},{6,14},{8,16},{10,18},{12,20},{14,22},{16,24},... | collective-permute-start | bytes 835592 | tf_op jit(solution)/shard_map/ppermute | solution.py:442
  54.8 1.6 %collective-permute-start.14 = (bf16[136,1024]{1,0:T(8,128)(2,1)S(1)}, bf16[136,1024]{1,0:T(8,128)(2,1)S(1)}, u32[]{:S(2)}, u32[]{:S(2)}) collective-permute-start(bf16[136,1024]{1,0:T(8,128)(2,1)S(1)} %collective-permute-done.13.x0), channel_id=1, source_target_pairs={{0,2},{2,0},{4,6},{6,4},{8,10},{10,8},{12,14},{14,12},{16,18},{18,... | collective-permute-start | bytes 835592 | tf_op jit(solution)/shard_map/ppermute | solution.py:442
  56.4 2.2 %copy-start.1 = (f32[512]{0:T(512)S(1)}, f32[512]{0:T(512)}, u32[]{:S(2)}) copy-start(f32[512]{0:T(512)} %param.18) | copy-start | bytes 6148
  56.4 2.2 %copy-start.2 = (f32[512]{0:T(512)S(1)}, f32[512]{0:T(512)}, u32[]{:S(2)}) copy-start(f32[512]{0:T(512)} %param.19) | copy-start | bytes 6148
where the time goes:
time: 70.4 us; the launch traced here: 70.3 us
  Pallas kernels  29.6 us (42%)
  waiting for transfers between devices  28.5 us (40%)
  starting transfers between devices  11.8 us (17%)
    ppermute x15, waiting for transfers between devices, send(): return lax.ppermute(value, 'seq', pairs(step, dy, dc))  28.5 us
    pallas_call x8, Pallas kernels, project(): pl.pallas_call(functools.partial(project_body, step, dy, outer), out_shap...  14.2 us
    ppermute x15, starting transfers between devices, send(): return lax.ppermute(value, 'seq', pairs(step, dy, dc))  11.8 us
    pallas_call x1, Pallas kernels, frames_call(): pl.pallas_call(frames_body, out_shape=jax.ShapeDtypeStruct((frames, chann...  11.5 us
    pallas_call x1, Pallas kernels, load(): pl.pallas_call(load_body, out_shape=(pltpu.VMEM(array.shape, array.dtype)...  2.86 us
  transfers between devices with their start and end apart: 15, of which 8 were waited for; matrix products, arithmetic and copies ran while one was open for 0% of the time, Pallas kernels for 21%

commit v1 on v0

--- a/solution.py
+++ b/solution.py
@@ -454,55 +454,94 @@
         return state, token
 
     w_qkv, token = load(where, w_qkv)
-    state = None
     far_up, far_down = outer // 2, (outer - 1) // 2
-    up = down = own = pack(where, units, durations[None, :], seg_ids[None, :])
-    arrived = [(0, own)]
-    waiting = []
-    for step in range(far_up + 1):
-        following = []
-        if step < far_up:
-            up = send(up, 1)
-            following.append((step + 1, up))
-        if step < far_down:
-            down = send(down, outer - 1)
-            following.append((-(step + 1), down))
+
+    def in_rounds(own, state, token):
+        up = down = own
+        arrived = [(0, own)]
+        waiting = []
+        for step in range(far_up + 1):
+            following = []
+            if step < far_up:
+                up = send(up, 1)
+                following.append((step + 1, up))
+            if step < far_down:
+                down = send(down, outer - 1)
+                following.append((-(step + 1), down))
+            for pair in waiting:
+                state, token = kernel(*pair, state, token)
+            if waiting and following:
+                held = lax.optimization_barrier((token, *[block for _, block in arrived]))
+                token = held[0]
+                arrived = [(d, block) for (d, _), block in zip(arrived, held[1:])]
+            sides = []
+            for d, block in arrived:
+                if step == far_up and step > 1:
+                    across = send(waiting_up, 1)
+                else:
+                    across = send(block, 0, 1, 0)
+                sides.append((d, block, across, send(block, 0, 0, 1)))
+            for d, block, across, beside in sides:
+                state, token = kernel(d, 0, (block, beside), state, token)
+            if step == 0:
+                ((d, _, across, _),) = sides
+                token, across = lax.optimization_barrier((token, across))
+                diagonal = send(across, 0, 0, 1)
+                state, token = kernel(d, 1, (across, diagonal), state, token)
+            halves = [across for _, _, across, _ in sides]
+            if following:
+                held = lax.optimization_barrier((token, *[block for _, block in following]))
+                token = held[0]
+                following = [(d, block) for (d, _), block in zip(following, held[1:])]
+                up = following[0][1]
+                down = following[1][1] if len(following) > 1 else None
+            waiting = []
+            for (d, _, _, _), across in zip(sides if step > 0 else (), halves):
+                token, across = lax.optimization_barrier((token, across))
+                waiting.append((d, 1, (across, send(across, 0, 0, 1))))
+            waiting_up = sides[0][2]
+            arrived = following
         for pair in waiting:
             state, token = kernel(*pair, state, token)
-        if waiting and following:
-            held = lax.optimization_barrier((token, *[block for _, block in arrived]))
-            token = held[0]
-            arrived = [(d, block) for (d, _), block in zip(arrived, held[1:])]
-        sides = []
-        for d, block in arrived:
-            if step == far_up and step > 1:
-                across = send(waiting_up, 1)
-            else:
-                across = send(block, 0, 1, 0)
-            sides.append((d, block, across, send(block, 0, 0, 1)))
-        for d, block, across, beside in sides:
-            state, token = kernel(d, 0, (block, beside), state, token)
-        if step == 0:
-            ((d, _, across, _),) = sides
-            token, across = lax.optimization_barrier((token, across))
-            diagonal = send(across, 0, 0, 1)
-            state, token = kernel(d, 1, (across, diagonal), state, token)
-        halves = [across for _, _, across, _ in sides]
-        if following:
-            held = lax.optimization_barrier((token, *[block for _, block in following]))
-            token = held[0]
-            following = [(d, block) for (d, _), block in zip(following, held[1:])]
-            up = following[0][1]
-            down = following[1][1] if len(following) > 1 else None
-        waiting = []
-        for (d, _, _, _), across in zip(sides if step > 0 else (), halves):
-            token, across = lax.optimization_barrier((token, across))
-            waiting.append((d, 1, (across, send(across, 0, 0, 1))))
-        waiting_up = sides[0][2]
-        arrived = following
-    for pair in waiting:
-        state, token = kernel(*pair, state, token)
-
+        return state
+
+    def four_planes(own, state, token):
+        def tie(token, *blocks):
+            return lax.optimization_barrier((token, *blocks))
+
+        up = send(own, 1)
+        across = send(own, 0, 1, 0)
+        beside = send(own, 0, 0, 1)
+        token, later = tie(token, own)
+        down = send(later, outer - 1)
+        state, token = kernel(0, 0, (own, beside), state, token)
+        token, up = tie(token, up)
+        far = send(up, 1)
+        up_across = send(up, 0, 1, 0)
+        up_beside = send(up, 0, 0, 1)
+        token, across = tie(token, across)
+        diagonal = send(across, 0, 0, 1)
+        state, token = kernel(1, 0, (up, up_beside), state, token)
+        state, token = kernel(0, 1, (across, diagonal), state, token)
+        token, down = tie(token, down)
+        down_across = send(down, 0, 1, 0)
+        down_beside = send(down, 0, 0, 1)
+        token, up_across = tie(token, up_across)
+        far_across = send(up_across, 1)
+        up_diagonal = send(up_across, 0, 0, 1)
+        far_beside = send(far, 0, 0, 1)
+        state, token = kernel(-1, 0, (down, down_beside), state, token)
+        state, token = kernel(1, 1, (up_across, up_diagonal), state, token)
+        state, token = kernel(2, 0, (far, far_beside), state, token)
+        token, down_across = tie(token, down_across)
+        down_diagonal = send(down_across, 0, 0, 1)
+        far_diagonal = send(far_across, 0, 0, 1)
+        state, token = kernel(-1, 1, (down_across, down_diagonal), state, token)
+        state, token = kernel(2, 1, (far_across, far_diagonal), state, token)
+        return state
+
+    own = pack(where, units, durations[None, :], seg_ids[None, :])
+    state = (four_planes if outer == 4 else in_rounds)(own, None, token)
     ks, vs, xa, meta = state
     return frames_call(
         where, meta, gain, conv_b[None, :], conv_gain[None, :], xa, ks, vs, w_qkv, w_out, w_proj,

time: 70.4 us -> 58 us (0.82)
  the two profiles are of different devices: /device:TPU:0 before, /device:TPU:1 now
where the time goes in v1:
time: 58 us; the launch traced here: 57.8 us
  Pallas kernels  29.6 us (51%)
  starting transfers between devices  14.4 us (25%)
  waiting for transfers between devices  13.4 us (23%)
    ppermute x15, starting transfers between devices, send(): return lax.ppermute(value, 'seq', pairs(step, dy, dc))  14.4 us
    pallas_call x8, Pallas kernels, project(): pl.pallas_call(functools.partial(project_body, step, dy, outer), out_shap...  14.2 us
    ppermute x15, waiting for transfers between devices, send(): return lax.ppermute(value, 'seq', pairs(step, dy, dc))  13.4 us
    pallas_call x1, Pallas kernels, frames_call(): pl.pallas_call(frames_body, out_shape=jax.ShapeDtypeStruct((frames, chann...  11.5 us
    pallas_call x1, Pallas kernels, load(): pl.pallas_call(load_body, out_shape=(pltpu.VMEM(array.shape, array.dtype)...  2.86 us
  transfers between devices with their start and end apart: 15, of which 5 were waited for; matrix products, arithmetic and copies ran while one was open for 0% of the time, Pallas kernels for 26%

profile of v1, /device:TPU:1, one launch (start us, length us, event | category | flops | bytes accessed | tf_op | source)
XLA Modules:
  0.0 57.8 jit_solution(7251967901430621425)
XLA Ops:
  0.0 0.0 copy-start
  0.0 1.0 %shard_map.100.x0 = bf16[136,1024]{1,0:T(8,128)(2,1)S(1)} custom-call(s32[1]{0:T(128)} %bitcast.here, bf16[128,1024]{1,0:T(8,128)(2,1)} %units.1, s32[1,128]{1,0:T(1,128)} %bitcast.17, s32[1,128]{1,0:T(1,128)} %bitcast.18), custom_call_target="tpu_custom_call" | custom-call | tf_op jit(solution)/shard_map/pallas_call | solution.py:64
  1.0 0.1 collective-permute-start
  1.1 2.8 %collective-permute-start.1 = (bf16[136,1024]{1,0:T(8,128)(2,1)S(1)}, bf16[136,1024]{1,0:T(8,128)(2,1)S(1)}, u32[]{:S(2)}, u32[]{:S(2)}) collective-permute-start(bf16[136,1024]{1,0:T(8,128)(2,1)S(1)} %shard_map.100.x0), channel_id=1, source_target_pairs={{0,8},{2,10},{4,12},{6,14},{8,16},{10,18},{12,20},{14,22},{16,24},... | collective-permute-start | bytes 835592 | tf_op jit(solution)/shard_map/ppermute | solution.py:442
  3.9 1.2 %collective-permute-start.2 = (bf16[136,1024]{1,0:T(8,128)(2,1)S(1)}, bf16[136,1024]{1,0:T(8,128)(2,1)S(1)}, u32[]{:S(2)}, u32[]{:S(2)}) collective-permute-start(bf16[136,1024]{1,0:T(8,128)(2,1)S(1)} %shard_map.100.x0), channel_id=1, source_target_pairs={{0,4},{2,6},{4,0},{6,2},{8,12},{10,14},{12,8},{14,10},{16,20},{18,... | collective-permute-start | bytes 835592 | tf_op jit(solution)/shard_map/ppermute | solution.py:442
  5.1 2.9 %shard_map.101 = (bf16[1024,3072]{1,0:T(8,128)(2,1)S(1)}, f32[8,128]{1,0:T(8,128)S(1)}) custom-call(s32[1]{0:T(128)} %bitcast.here, bf16[1024,3072]{1,0:T(8,128)(2,1)} %source.1), custom_call_target="tpu_custom_call" | custom-call | bytes 12582912 | tf_op jit(solution)/shard_map/pallas_call | solution.py:126
  8.0 0.0 collective-permute-done.x1
  8.0 0.0 copy-done
  8.0 1.7 %shard_map.102 = (bf16[8,256,1024]{2,1,0:T(8,128)(2,1)S(1)}, bf16[8,1024,256]{2,1,0:T(8,128)(2,1)S(1)}, bf16[2048,1024]{1,0:T(8,128)(2,1)S(1)}, bf16[16,8,256]{2,1,0:T(8,128)(2,1)S(1)}, f32[8,128]{1,0:T(8,128)S(1)}) custom-call(s32[1]{0:T(128)} %bitcast.here, bf16[136,1024]{1,0:T(8,128)(2,1)S(1)} %shard_map.100.x0, ...), custom_call_target="tpu_custom_call" | custom-call | flops 1073741824 | bytes 6291456 | tf_op jit(solution)/shard_map/pallas_call | solution.py:187
  9.7 3.1 %collective-permute-done.1.x0 = bf16[136,1024]{1,0:T(8,128)(2,1)S(1)} collective-permute-done((bf16[136,1024]{1,0:T(8,128)(2,1)S(1)}, bf16[136,1024]{1,0:T(8,128)(2,1)S(1)}, u32[]{:S(2)}, u32[]{:S(2)}) %collective-permute-start.1) | collective-permute-done | bytes 278560 | tf_op jit(solution)/shard_map/ppermute | solution.py:442
  12.9 0.6 %collective-permute-start.4 = (bf16[136,1024]{1,0:T(8,128)(2,1)S(1)}, bf16[136,1024]{1,0:T(8,128)(2,1)S(1)}, u32[]{:S(2)}, u32[]{:S(2)}) collective-permute-start(bf16[136,1024]{1,0:T(8,128)(2,1)S(1)} %collective-permute-done.1.x0), channel_id=1, source_target_pairs={{0,2},{2,0},{4,6},{6,4},{8,10},{10,8},{12,14},{14,12},{16,18},{18,... | collective-permute-start | bytes 835592 | tf_op jit(solution)/shard_map/ppermute | solution.py:442
  13.5 0.0 collective-permute-done.2.x0
  13.5 0.0 collective-permute-start.3
  13.5 1.5 %collective-permute-start.5 = (bf16[136,1024]{1,0:T(8,128)(2,1)S(1)}, bf16[136,1024]{1,0:T(8,128)(2,1)S(1)}, u32[]{:S(2)}, u32[]{:S(2)}) collective-permute-start(bf16[136,1024]{1,0:T(8,128)(2,1)S(1)} %shard_map.100.x0), channel_id=1, source_target_pairs={{0,24},{2,26},{4,28},{6,30},{8,0},{10,2},{12,4},{14,6},{16,8},{18,... | collective-permute-start | bytes 835592 | tf_op jit(solution)/shard_map/ppermute | solution.py:442
  15.0 1.2 %collective-permute-start.6 = (bf16[136,1024]{1,0:T(8,128)(2,1)S(1)}, bf16[136,1024]{1,0:T(8,128)(2,1)S(1)}, u32[]{:S(2)}, u32[]{:S(2)}) collective-permute-start(bf16[136,1024]{1,0:T(8,128)(2,1)S(1)} %collective-permute-done.1.x0), channel_id=1, source_target_pairs={{0,4},{2,6},{4,0},{6,2},{8,12},{10,14},{12,8},{14,10},{16,20},{18,... | collective-permute-start | bytes 835592 | tf_op jit(solution)/shard_map/ppermute | solution.py:442
  16.2 0.0 collective-permute-start.9
  16.2 0.0 collective-permute-done.4.x1
  16.2 1.7 %shard_map.103 = (bf16[8,256,1024]{2,1,0:T(8,128)(2,1)S(1)}, bf16[8,1024,256]{2,1,0:T(8,128)(2,1)S(1)}, bf16[2048,1024]{1,0:T(8,128)(2,1)S(1)}, bf16[16,8,256]{2,1,0:T(8,128)(2,1)S(1)}, f32[8,128]{1,0:T(8,128)S(1)}) custom-call(s32[1]{0:T(128)} %bitcast.here, ...), custom_call_target="tpu_custom_call", output_to_operand_aliasing={{0}: (6, {}), {1}: (7, {}), {2}: (8, {}), {3}: (9, {})} | custom-call | flops 1073741824 | bytes 6291456 | tf_op jit(solution)/shard_map/pallas_call | solution.py:187
  17.9 0.0 collective-permute-done.3.x1
  18.0 1.7 %shard_map.104 = (bf16[8,256,1024]{2,1,0:T(8,128)(2,1)S(1)}, bf16[8,1024,256]{2,1,0:T(8,128)(2,1)S(1)}, bf16[2048,1024]{1,0:T(8,128)(2,1)S(1)}, bf16[16,8,256]{2,1,0:T(8,128)(2,1)S(1)}, f32[8,128]{1,0:T(8,128)S(1)}) custom-call(s32[1]{0:T(128)} %bitcast.here, ...), custom_call_target="tpu_custom_call", output_to_operand_aliasing={{0}: (6, {}), {1}: (7, {}), {2}: (8, {}), {3}: (9, {})} | custom-call | flops 1073741824 | bytes 6291456 | tf_op jit(solution)/shard_map/pallas_call | solution.py:187
  19.7 1.5 %collective-permute-done.5.x0 = bf16[136,1024]{1,0:T(8,128)(2,1)S(1)} collective-permute-done((bf16[136,1024]{1,0:T(8,128)(2,1)S(1)}, bf16[136,1024]{1,0:T(8,128)(2,1)S(1)}, u32[]{:S(2)}, u32[]{:S(2)}) %collective-permute-start.5) | collective-permute-done | bytes 278560 | tf_op jit(solution)/shard_map/ppermute | solution.py:442
  21.2 1.6 %collective-permute-start.12 = (bf16[136,1024]{1,0:T(8,128)(2,1)S(1)}, bf16[136,1024]{1,0:T(8,128)(2,1)S(1)}, u32[]{:S(2)}, u32[]{:S(2)}) collective-permute-start(bf16[136,1024]{1,0:T(8,128)(2,1)S(1)} %collective-permute-done.5.x0), channel_id=1, source_target_pairs={{0,2},{2,0},{4,6},{6,4},{8,10},{10,8},{12,14},{14,12},{16,18},{18,... | collective-permute-start | bytes 835592 | tf_op jit(solution)/shard_map/ppermute | solution.py:442
  22.9 0.0 collective-permute-done.6.x0
  22.9 1.2 %collective-permute-start.11 = (bf16[136,1024]{1,0:T(8,128)(2,1)S(1)}, bf16[136,1024]{1,0:T(8,128)(2,1)S(1)}, u32[]{:S(2)}, u32[]{:S(2)}) collective-permute-start(bf16[136,1024]{1,0:T(8,128)(2,1)S(1)} %collective-permute-done.6.x0), channel_id=1, source_target_pairs={{0,2},{2,0},{4,6},{6,4},{8,10},{10,8},{12,14},{14,12},{16,18},{18,... | collective-permute-start | bytes 835592 | tf_op jit(solution)/shard_map/ppermute | solution.py:442
  24.1 5.1 %collective-permute-done.9.x0 = bf16[136,1024]{1,0:T(8,128)(2,1)S(1)} collective-permute-done((bf16[136,1024]{1,0:T(8,128)(2,1)S(1)}, bf16[136,1024]{1,0:T(8,128)(2,1)S(1)}, u32[]{:S(2)}, u32[]{:S(2)}) %collective-permute-start.9) | collective-permute-done | bytes 278560 | tf_op jit(solution)/shard_map/ppermute | solution.py:442
  29.2 0.9 %collective-permute-start.10 = (bf16[136,1024]{1,0:T(8,128)(2,1)S(1)}, bf16[136,1024]{1,0:T(8,128)(2,1)S(1)}, u32[]{:S(2)}, u32[]{:S(2)}) collective-permute-start(bf16[136,1024]{1,0:T(8,128)(2,1)S(1)} %collective-permute-done.9.x0), channel_id=1, source_target_pairs={{0,2},{2,0},{4,6},{6,4},{8,10},{10,8},{12,14},{14,12},{16,18},{18,... | collective-permute-start | bytes 835592 | tf_op jit(solution)/shard_map/ppermute | solution.py:442
  30.0 1.2 %collective-permute-start.13 = (bf16[136,1024]{1,0:T(8,128)(2,1)S(1)}, bf16[136,1024]{1,0:T(8,128)(2,1)S(1)}, u32[]{:S(2)}, u32[]{:S(2)}) collective-permute-start(bf16[136,1024]{1,0:T(8,128)(2,1)S(1)} %collective-permute-done.5.x0), channel_id=1, source_target_pairs={{0,4},{2,6},{4,0},{6,2},{8,12},{10,14},{12,8},{14,10},{16,20},{18,... | collective-permute-start | bytes 835592 | tf_op jit(solution)/shard_map/ppermute | solution.py:442
  31.3 0.1 collective-permute-start.7
  31.3 0.0 collective-permute-done.12.x1
  31.3 1.7 %shard_map.105 = (bf16[8,256,1024]{2,1,0:T(8,128)(2,1)S(1)}, bf16[8,1024,256]{2,1,0:T(8,128)(2,1)S(1)}, bf16[2048,1024]{1,0:T(8,128)(2,1)S(1)}, bf16[16,8,256]{2,1,0:T(8,128)(2,1)S(1)}, f32[8,128]{1,0:T(8,128)S(1)}) custom-call(s32[1]{0:T(128)} %bitcast.here, ...), custom_call_target="tpu_custom_call", output_to_operand_aliasing={{0}: (6, {}), {1}: (7, {}), {2}: (8, {}), {3}: (9, {})} | custom-call | flops 1073741824 | bytes 6291456 | tf_op jit(solution)/shard_map/pallas_call | solution.py:187
  33.0 0.0 collective-permute-done.11.x1
  33.0 1.7 %shard_map.106 = (bf16[8,256,1024]{2,1,0:T(8,128)(2,1)S(1)}, bf16[8,1024,256]{2,1,0:T(8,128)(2,1)S(1)}, bf16[2048,1024]{1,0:T(8,128)(2,1)S(1)}, bf16[16,8,256]{2,1,0:T(8,128)(2,1)S(1)}, f32[8,128]{1,0:T(8,128)S(1)}) custom-call(s32[1]{0:T(128)} %bitcast.here, ...), custom_call_target="tpu_custom_call", output_to_operand_aliasing={{0}: (6, {}), {1}: (7, {}), {2}: (8, {}), {3}: (9, {})} | custom-call | flops 1073741824 | bytes 6291456 | tf_op jit(solution)/shard_map/pallas_call | solution.py:187
  34.8 0.0 collective-permute-done.10.x1
  34.8 1.7 %shard_map.107 = (bf16[8,256,1024]{2,1,0:T(8,128)(2,1)S(1)}, bf16[8,1024,256]{2,1,0:T(8,128)(2,1)S(1)}, bf16[2048,1024]{1,0:T(8,128)(2,1)S(1)}, bf16[16,8,256]{2,1,0:T(8,128)(2,1)S(1)}, f32[8,128]{1,0:T(8,128)S(1)}) custom-call(s32[1]{0:T(128)} %bitcast.here, ...), custom_call_target="tpu_custom_call", output_to_operand_aliasing={{0}: (6, {}), {1}: (7, {}), {2}: (8, {}), {3}: (9, {})} | custom-call | flops 1073741824 | bytes 6291456 | tf_op jit(solution)/shard_map/pallas_call | solution.py:187
  36.5 1.7 %collective-permute-done.13.x0 = bf16[136,1024]{1,0:T(8,128)(2,1)S(1)} collective-permute-done((bf16[136,1024]{1,0:T(8,128)(2,1)S(1)}, bf16[136,1024]{1,0:T(8,128)(2,1)S(1)}, u32[]{:S(2)}, u32[]{:S(2)}) %collective-permute-start.13) | collective-permute-done | bytes 278560 | tf_op jit(solution)/shard_map/ppermute | solution.py:442
  38.2 0.9 %collective-permute-start.14 = (bf16[136,1024]{1,0:T(8,128)(2,1)S(1)}, bf16[136,1024]{1,0:T(8,128)(2,1)S(1)}, u32[]{:S(2)}, u32[]{:S(2)}) collective-permute-start(bf16[136,1024]{1,0:T(8,128)(2,1)S(1)} %collective-permute-done.13.x0), channel_id=1, source_target_pairs={{0,2},{2,0},{4,6},{6,4},{8,10},{10,8},{12,14},{14,12},{16,18},{18,... | collective-permute-start | bytes 835592 | tf_op jit(solution)/shard_map/ppermute | solution.py:442
  39.1 1.9 %collective-permute-done.7.x0 = bf16[136,1024]{1,0:T(8,128)(2,1)S(1)} collective-permute-done((bf16[136,1024]{1,0:T(8,128)(2,1)S(1)}, bf16[136,1024]{1,0:T(8,128)(2,1)S(1)}, u32[]{:S(2)}, u32[]{:S(2)}) %collective-permute-start.7) | collective-permute-done | bytes 278560 | tf_op jit(solution)/shard_map/ppermute | solution.py:442
  41.0 1.1 %collective-permute-start.8 = (bf16[136,1024]{1,0:T(8,128)(2,1)S(1)}, bf16[136,1024]{1,0:T(8,128)(2,1)S(1)}, u32[]{:S(2)}, u32[]{:S(2)}) collective-permute-start(bf16[136,1024]{1,0:T(8,128)(2,1)S(1)} %collective-permute-done.7.x0), channel_id=1, source_target_pairs={{0,2},{2,0},{4,6},{6,4},{8,10},{10,8},{12,14},{14,12},{16,18},{18,... | collective-permute-start | bytes 835592 | tf_op jit(solution)/shard_map/ppermute | solution.py:442
  42.1 0.0 collective-permute-done.14.x1
  42.1 1.7 %shard_map.108 = (bf16[8,256,1024]{2,1,0:T(8,128)(2,1)S(1)}, bf16[8,1024,256]{2,1,0:T(8,128)(2,1)S(1)}, bf16[2048,1024]{1,0:T(8,128)(2,1)S(1)}, bf16[16,8,256]{2,1,0:T(8,128)(2,1)S(1)}, f32[8,128]{1,0:T(8,128)S(1)}) custom-call(s32[1]{0:T(128)} %bitcast.here, ...), custom_call_target="tpu_custom_call", output_to_operand_aliasing={{0}: (6, {}), {1}: (7, {}), {2}: (8, {}), {3}: (9, {})} | custom-call | flops 1073741824 | bytes 6291456 | tf_op jit(solution)/shard_map/pallas_call | solution.py:187
  43.9 0.0 collective-permute-done.8.x1
  43.9 0.0 copy-start.1
  43.9 0.0 copy-start.2
  43.9 2.2 %shard_map.109 = (bf16[8,256,1024]{2,1,0:T(8,128)(2,1)S(1)}, bf16[8,1024,256]{2,1,0:T(8,128)(2,1)S(1)}, bf16[2048,1024]{1,0:T(8,128)(2,1)S(1)}, bf16[16,8,256]{2,1,0:T(8,128)(2,1)S(1)}, f32[8,128]{1,0:T(8,128)}) custom-call(s32[1]{0:T(128)} %bitcast.here, ...), custom_call_target="tpu_custom_call", output_to_operand_aliasing={{0}: (6, {}), {1}: (7, {}), {2}: (8, {}), {3}: (9, {})} | custom-call | flops 1073741824 | bytes 6291456 | tf_op jit(solution)/shard_map/pallas_call | solution.py:187
  46.1 0.0 copy-done.1
  46.1 0.0 copy-done.2
  46.1 11.5 %shard_map.110 = bf16[768,512]{1,0:T(8,128)(2,1)} custom-call(s32[1]{0:T(128)} %bitcast.here, bf16[16,8,256]{2,1,0:T(8,128)(2,1)S(1)} %get-tuple-element.107.meta, f32[1,1024]{1,0:T(1,128)S(1)} %bitcast.14, f32[1,512]{1,0:T(1,128)S(1)} %bitcast.15, f32[1,512]{1,0:T(1,128)S(1)} %bitcast.16, bf16[2048,1024]{1,0:T(8,128)(2,1)S(1)} %get-tuple-element.108.xa, ...), custom_call_target="tpu_custom_call" | custom-call | tf_op jit(solution)/shard_map/pallas_call | solution.py:392
Async XLA Ops:
  0.0 8.0 %copy-start = (f32[1024]{0:T(1024)S(1)}, f32[1024]{0:T(1024)}, u32[]{:S(2)}) copy-start(f32[1024]{0:T(1024)} %param.13) | copy-start | bytes 12292
  1.0 7.0 %collective-permute-start = (bf16[136,1024]{1,0:T(8,128)(2,1)S(1)}, bf16[136,1024]{1,0:T(8,128)(2,1)S(1)}, u32[]{:S(2)}, u32[]{:S(2)}) collective-permute-start(bf16[136,1024]{1,0:T(8,128)(2,1)S(1)} %shard_map.100.x0), channel_id=1, source_target_pairs={{0,2},{2,0},{4,6},{6,4},{8,10},{10,8},{12,14},{14,12},{16,18},{18,... | collective-permute-start | bytes 835592 | tf_op jit(solution)/shard_map/ppermute | solution.py:442
  1.1 11.8 %collective-permute-start.1 = (bf16[136,1024]{1,0:T(8,128)(2,1)S(1)}, bf16[136,1024]{1,0:T(8,128)(2,1)S(1)}, u32[]{:S(2)}, u32[]{:S(2)}) collective-permute-start(bf16[136,1024]{1,0:T(8,128)(2,1)S(1)} %shard_map.100.x0), channel_id=1, source_target_pairs={{0,8},{2,10},{4,12},{6,14},{8,16},{10,18},{12,20},{14,22},{16,24},... | collective-permute-start | bytes 835592 | tf_op jit(solution)/shard_map/ppermute | solution.py:442
  3.9 9.6 %collective-permute-start.2 = (bf16[136,1024]{1,0:T(8,128)(2,1)S(1)}, bf16[136,1024]{1,0:T(8,128)(2,1)S(1)}, u32[]{:S(2)}, u32[]{:S(2)}) collective-permute-start(bf16[136,1024]{1,0:T(8,128)(2,1)S(1)} %shard_map.100.x0), channel_id=1, source_target_pairs={{0,4},{2,6},{4,0},{6,2},{8,12},{10,14},{12,8},{14,10},{16,20},{18,... | collective-permute-start | bytes 835592 | tf_op jit(solution)/shard_map/ppermute | solution.py:442
  12.9 3.4 %collective-permute-start.4 = (bf16[136,1024]{1,0:T(8,128)(2,1)S(1)}, bf16[136,1024]{1,0:T(8,128)(2,1)S(1)}, u32[]{:S(2)}, u32[]{:S(2)}) collective-permute-start(bf16[136,1024]{1,0:T(8,128)(2,1)S(1)} %collective-permute-done.1.x0), channel_id=1, source_target_pairs={{0,2},{2,0},{4,6},{6,4},{8,10},{10,8},{12,14},{14,12},{16,18},{18,... | collective-permute-start | bytes 835592 | tf_op jit(solution)/shard_map/ppermute | solution.py:442
  13.5 4.4 %collective-permute-start.3 = (bf16[136,1024]{1,0:T(8,128)(2,1)S(1)}, bf16[136,1024]{1,0:T(8,128)(2,1)S(1)}, u32[]{:S(2)}, u32[]{:S(2)}) collective-permute-start(bf16[136,1024]{1,0:T(8,128)(2,1)S(1)} %collective-permute-done.2.x0), channel_id=1, source_target_pairs={{0,2},{2,0},{4,6},{6,4},{8,10},{10,8},{12,14},{14,12},{16,18},{18,... | collective-permute-start | bytes 835592 | tf_op jit(solution)/shard_map/ppermute | solution.py:442
  13.5 7.7 %collective-permute-start.5 = (bf16[136,1024]{1,0:T(8,128)(2,1)S(1)}, bf16[136,1024]{1,0:T(8,128)(2,1)S(1)}, u32[]{:S(2)}, u32[]{:S(2)}) collective-permute-start(bf16[136,1024]{1,0:T(8,128)(2,1)S(1)} %shard_map.100.x0), channel_id=1, source_target_pairs={{0,24},{2,26},{4,28},{6,30},{8,0},{10,2},{12,4},{14,6},{16,8},{18,... | collective-permute-start | bytes 835592 | tf_op jit(solution)/shard_map/ppermute | solution.py:442
  15.0 7.9 %collective-permute-start.6 = (bf16[136,1024]{1,0:T(8,128)(2,1)S(1)}, bf16[136,1024]{1,0:T(8,128)(2,1)S(1)}, u32[]{:S(2)}, u32[]{:S(2)}) collective-permute-start(bf16[136,1024]{1,0:T(8,128)(2,1)S(1)} %collective-permute-done.1.x0), channel_id=1, source_target_pairs={{0,4},{2,6},{4,0},{6,2},{8,12},{10,14},{12,8},{14,10},{16,20},{18,... | collective-permute-start | bytes 835592 | tf_op jit(solution)/shard_map/ppermute | solution.py:442
  16.2 12.9 %collective-permute-start.9 = (bf16[136,1024]{1,0:T(8,128)(2,1)S(1)}, bf16[136,1024]{1,0:T(8,128)(2,1)S(1)}, u32[]{:S(2)}, u32[]{:S(2)}) collective-permute-start(bf16[136,1024]{1,0:T(8,128)(2,1)S(1)} %collective-permute-done.1.x0), channel_id=1, source_target_pairs={{0,8},{2,10},{4,12},{6,14},{8,16},{10,18},{12,20},{14,22},{16,24},... | collective-permute-start | bytes 835592 | tf_op jit(solution)/shard_map/ppermute | solution.py:442
  21.2 10.1 %collective-permute-start.12 = (bf16[136,1024]{1,0:T(8,128)(2,1)S(1)}, bf16[136,1024]{1,0:T(8,128)(2,1)S(1)}, u32[]{:S(2)}, u32[]{:S(2)}) collective-permute-start(bf16[136,1024]{1,0:T(8,128)(2,1)S(1)} %collective-permute-done.5.x0), channel_id=1, source_target_pairs={{0,2},{2,0},{4,6},{6,4},{8,10},{10,8},{12,14},{14,12},{16,18},{18,... | collective-permute-start | bytes 835592 | tf_op jit(solution)/shard_map/ppermute | solution.py:442
  22.9 10.2 %collective-permute-start.11 = (bf16[136,1024]{1,0:T(8,128)(2,1)S(1)}, bf16[136,1024]{1,0:T(8,128)(2,1)S(1)}, u32[]{:S(2)}, u32[]{:S(2)}) collective-permute-start(bf16[136,1024]{1,0:T(8,128)(2,1)S(1)} %collective-permute-done.6.x0), channel_id=1, source_target_pairs={{0,2},{2,0},{4,6},{6,4},{8,10},{10,8},{12,14},{14,12},{16,18},{18,... | collective-permute-start | bytes 835592 | tf_op jit(solution)/shard_map/ppermute | solution.py:442
  29.2 5.6 %collective-permute-start.10 = (bf16[136,1024]{1,0:T(8,128)(2,1)S(1)}, bf16[136,1024]{1,0:T(8,128)(2,1)S(1)}, u32[]{:S(2)}, u32[]{:S(2)}) collective-permute-start(bf16[136,1024]{1,0:T(8,128)(2,1)S(1)} %collective-permute-done.9.x0), channel_id=1, source_target_pairs={{0,2},{2,0},{4,6},{6,4},{8,10},{10,8},{12,14},{14,12},{16,18},{18,... | collective-permute-start | bytes 835592 | tf_op jit(solution)/shard_map/ppermute | solution.py:442
  30.0 8.2 %collective-permute-start.13 = (bf16[136,1024]{1,0:T(8,128)(2,1)S(1)}, bf16[136,1024]{1,0:T(8,128)(2,1)S(1)}, u32[]{:S(2)}, u32[]{:S(2)}) collective-permute-start(bf16[136,1024]{1,0:T(8,128)(2,1)S(1)} %collective-permute-done.5.x0), channel_id=1, source_target_pairs={{0,4},{2,6},{4,0},{6,2},{8,12},{10,14},{12,8},{14,10},{16,20},{18,... | collective-permute-start | bytes 835592 | tf_op jit(solution)/shard_map/ppermute | solution.py:442
  31.3 9.7 %collective-permute-start.7 = (bf16[136,1024]{1,0:T(8,128)(2,1)S(1)}, bf16[136,1024]{1,0:T(8,128)(2,1)S(1)}, u32[]{:S(2)}, u32[]{:S(2)}) collective-permute-start(bf16[136,1024]{1,0:T(8,128)(2,1)S(1)} %collective-permute-done.6.x0), channel_id=1, source_target_pairs={{0,8},{2,10},{4,12},{6,14},{8,16},{10,18},{12,20},{14,22},{16,24},... | collective-permute-start | bytes 835592 | tf_op jit(solution)/shard_map/ppermute | solution.py:442
  38.2 3.9 %collective-permute-start.14 = (bf16[136,1024]{1,0:T(8,128)(2,1)S(1)}, bf16[136,1024]{1,0:T(8,128)(2,1)S(1)}, u32[]{:S(2)}, u32[]{:S(2)}) collective-permute-start(bf16[136,1024]{1,0:T(8,128)(2,1)S(1)} %collective-permute-done.13.x0), channel_id=1, source_target_pairs={{0,2},{2,0},{4,6},{6,4},{8,10},{10,8},{12,14},{14,12},{16,18},{18,... | collective-permute-start | bytes 835592 | tf_op jit(solution)/shard_map/ppermute | solution.py:442
  41.0 2.9 %collective-permute-start.8 = (bf16[136,1024]{1,0:T(8,128)(2,1)S(1)}, bf16[136,1024]{1,0:T(8,128)(2,1)S(1)}, u32[]{:S(2)}, u32[]{:S(2)}) collective-permute-start(bf16[136,1024]{1,0:T(8,128)(2,1)S(1)} %collective-permute-done.7.x0), channel_id=1, source_target_pairs={{0,2},{2,0},{4,6},{6,4},{8,10},{10,8},{12,14},{14,12},{16,18},{18,... | collective-permute-start | bytes 835592 | tf_op jit(solution)/shard_map/ppermute | solution.py:442
  43.9 2.3 %copy-start.1 = (f32[512]{0:T(512)S(1)}, f32[512]{0:T(512)}, u32[]{:S(2)}) copy-start(f32[512]{0:T(512)} %param.18) | copy-start | bytes 6148
  43.9 2.3 %copy-start.2 = (f32[512]{0:T(512)S(1)}, f32[512]{0:T(512)}, u32[]{:S(2)}) copy-start(f32[512]{0:T(512)} %param.19) | copy-start | bytes 6148

commit v2 on v1

--- a/solution.py
+++ b/solution.py
@@ -281,36 +281,35 @@
         def key_step(t, c):
             key = t * tile + lax.broadcasted_iota(jnp.int32, (tile, 2 * MAIN), 0)
             bias[...] = jnp.where((key >= row_lo) & (key < row_hi), 0.0, MASKED)
-            main = bias[:, :MAIN]
-            mask = jnp.concatenate([main] * GROUP + [bias[:, MAIN:]], axis=1)
             groups = HEADS // GROUP
 
             ahead = begun[...]
             for g in range(groups):
                 dims = slice(g * deep, (g + 1) * deep)
-                s = ahead * scale + mask
+                now = ahead
                 if g + 1 < groups:
                     ahead = scores(t, g + 1)
                 else:
                     begun[...] = scores(jnp.minimum(t + 1, t1 - 1), 0)
-                top = tops[g]
-                new_top = jnp.maximum(top, jnp.max(s, axis=0, keepdims=True))
-                expo = jnp.exp2(s - new_top)
-                alpha = jnp.exp2(top - new_top)
-                tops[g] = new_top
-                totals[g] = totals[g] * alpha + jnp.sum(expo, axis=0, keepdims=True)
-                expo = expo.astype(jnp.bfloat16)
-                for j in range(GROUP):
+                for j in range(GROUP + 1):
                     lanes = slice(j * MAIN, (j + 1) * MAIN)
-                    start = g * deep + j * head
-                    acc[g, j] = acc[g, j] * alpha[:, lanes] + jnp.dot(
-                        values[t, start : start + head, :], expo[:, lanes],
-                        preferred_element_type=jnp.float32,
-                    )
-                acc_rest[g] = acc_rest[g] * alpha[:, GROUP * MAIN :] + jnp.dot(
-                    values[t, dims, :], expo[:, GROUP * MAIN :],
-                    preferred_element_type=jnp.float32,
-                )
+                    s = now[:, lanes] * scale + (bias[:, :MAIN] if j < GROUP else bias[:, MAIN:])
+                    top = tops[g][:, lanes]
+                    new_top = jnp.maximum(top, jnp.max(s, axis=0, keepdims=True))
+                    expo = jnp.exp2(s - new_top)
+                    alpha = jnp.exp2(top - new_top)
+                    tops[g, :, lanes] = new_top
+                    totals[g, :, lanes] = totals[g][:, lanes] * alpha + jnp.sum(expo, axis=0, keepdims=True)
+                    expo = expo.astype(jnp.bfloat16)
+                    if j < GROUP:
+                        start = g * deep + j * head
+                        acc[g, j] = acc[g, j] * alpha + jnp.dot(
+                            values[t, start : start + head, :], expo, preferred_element_type=jnp.float32
+                        )
+                    else:
+                        acc_rest[g] = acc_rest[g] * alpha + jnp.dot(
+                            values[t, dims, :], expo, preferred_element_type=jnp.float32
+                        )
             return c
 
         lax.fori_loop(t0, t1, key_step, 0)
@@ -529,14 +528,16 @@
         token, up_across = tie(token, up_across)
         far_across = send(up_across, 1)
         up_diagonal = send(up_across, 0, 0, 1)
-        far_beside = send(far, 0, 0, 1)
         state, token = kernel(-1, 0, (down, down_beside), state, token)
         state, token = kernel(1, 1, (up_across, up_diagonal), state, token)
-        state, token = kernel(2, 0, (far, far_beside), state, token)
+        token, far = tie(token, far)
+        far_beside = send(far, 0, 0, 1)
         token, down_across = tie(token, down_across)
         down_diagonal = send(down_across, 0, 0, 1)
+        state, token = kernel(2, 0, (far, far_beside), state, token)
+        state, token = kernel(-1, 1, (down_across, down_diagonal), state, token)
+        token, far_across = tie(token, far_across)
         far_diagonal = send(far_across, 0, 0, 1)
-        state, token = kernel(-1, 1, (down_across, down_diagonal), state, token)
         state, token = kernel(2, 1, (far_across, far_diagonal), state, token)
         return state
 

time: 58 us -> 61.2 us (1.055)
  the two profiles are of different devices: /device:TPU:1 before, /device:TPU:0 now
where the time goes in v2:
time: 61.2 us; the launch traced here: 61.1 us
  Pallas kernels  29.4 us (48%)
  waiting for transfers between devices  20.6 us (34%)
  starting transfers between devices  10.8 us (18%)
    ppermute x15, waiting for transfers between devices, send(): return lax.ppermute(value, 'seq', pairs(step, dy, dc))  20.6 us
    pallas_call x8, Pallas kernels, project(): pl.pallas_call(functools.partial(project_body, step, dy, outer), out_shap...  14.2 us
    pallas_call x1, Pallas kernels, frames_call(): pl.pallas_call(frames_body, out_shape=jax.ShapeDtypeStruct((frames, chann...  11.3 us
    ppermute x15, starting transfers between devices, send(): return lax.ppermute(value, 'seq', pairs(step, dy, dc))  10.8 us
    pallas_call x1, Pallas kernels, load(): pl.pallas_call(load_body, out_shape=(pltpu.VMEM(array.shape, array.dtype)...  2.86 us
  transfers between devices with their start and end apart: 15, of which 7 were waited for; matrix products, arithmetic and copies ran while one was open for 0% of the time, Pallas kernels for 24%

profile of v2, /device:TPU:0, one launch (start us, length us, event | category | flops | bytes accessed | tf_op | source)
XLA Modules:
  0.0 61.1 jit_solution(16053379413310396391)
XLA Ops:
  0.0 0.0 copy-start
  0.0 1.0 %shard_map.100.x0 = bf16[136,1024]{1,0:T(8,128)(2,1)S(1)} custom-call(s32[1]{0:T(128)} %bitcast.here, bf16[128,1024]{1,0:T(8,128)(2,1)} %units.1, s32[1,128]{1,0:T(1,128)} %bitcast.17, s32[1,128]{1,0:T(1,128)} %bitcast.18), custom_call_target="tpu_custom_call" | custom-call | tf_op jit(solution)/shard_map/pallas_call | solution.py:64
  1.0 0.6 collective-permute-start
  1.6 2.6 %collective-permute-start.1 = (bf16[136,1024]{1,0:T(8,128)(2,1)S(1)}, bf16[136,1024]{1,0:T(8,128)(2,1)S(1)}, u32[]{:S(2)}, u32[]{:S(2)}) collective-permute-start(bf16[136,1024]{1,0:T(8,128)(2,1)S(1)} %shard_map.100.x0), channel_id=1, source_target_pairs={{0,8},{2,10},{4,12},{6,14},{8,16},{10,18},{12,20},{14,22},{16,24},... | collective-permute-start | bytes 835592 | tf_op jit(solution)/shard_map/ppermute | solution.py:441
  4.2 1.5 %collective-permute-start.2 = (bf16[136,1024]{1,0:T(8,128)(2,1)S(1)}, bf16[136,1024]{1,0:T(8,128)(2,1)S(1)}, u32[]{:S(2)}, u32[]{:S(2)}) collective-permute-start(bf16[136,1024]{1,0:T(8,128)(2,1)S(1)} %shard_map.100.x0), channel_id=1, source_target_pairs={{0,4},{2,6},{4,0},{6,2},{8,12},{10,14},{12,8},{14,10},{16,20},{18,... | collective-permute-start | bytes 835592 | tf_op jit(solution)/shard_map/ppermute | solution.py:441
  5.7 2.9 %shard_map.101 = (bf16[1024,3072]{1,0:T(8,128)(2,1)S(1)}, f32[8,128]{1,0:T(8,128)S(1)}) custom-call(s32[1]{0:T(128)} %bitcast.here, bf16[1024,3072]{1,0:T(8,128)(2,1)} %source.1), custom_call_target="tpu_custom_call" | custom-call | bytes 12582912 | tf_op jit(solution)/shard_map/pallas_call | solution.py:126
  8.6 0.0 collective-permute-done.x1
  8.6 0.0 copy-done
  8.6 1.7 %shard_map.102 = (bf16[8,256,1024]{2,1,0:T(8,128)(2,1)S(1)}, bf16[8,1024,256]{2,1,0:T(8,128)(2,1)S(1)}, bf16[2048,1024]{1,0:T(8,128)(2,1)S(1)}, bf16[16,8,256]{2,1,0:T(8,128)(2,1)S(1)}, f32[8,128]{1,0:T(8,128)S(1)}) custom-call(s32[1]{0:T(128)} %bitcast.here, bf16[136,1024]{1,0:T(8,128)(2,1)S(1)} %shard_map.100.x0, ...), custom_call_target="tpu_custom_call" | custom-call | flops 1073741824 | bytes 6291456 | tf_op jit(solution)/shard_map/pallas_call | solution.py:187
  10.4 3.2 %collective-permute-done.1.x0 = bf16[136,1024]{1,0:T(8,128)(2,1)S(1)} collective-permute-done((bf16[136,1024]{1,0:T(8,128)(2,1)S(1)}, bf16[136,1024]{1,0:T(8,128)(2,1)S(1)}, u32[]{:S(2)}, u32[]{:S(2)}) %collective-permute-start.1) | collective-permute-done | bytes 278560 | tf_op jit(solution)/shard_map/ppermute | solution.py:441
  13.5 0.0 collective-permute-start.4
  13.5 0.0 collective-permute-done.2.x0
  13.5 0.5 collective-permute-start.3
  14.0 1.7 %collective-permute-start.5 = (bf16[136,1024]{1,0:T(8,128)(2,1)S(1)}, bf16[136,1024]{1,0:T(8,128)(2,1)S(1)}, u32[]{:S(2)}, u32[]{:S(2)}) collective-permute-start(bf16[136,1024]{1,0:T(8,128)(2,1)S(1)} %shard_map.100.x0), channel_id=1, source_target_pairs={{0,24},{2,26},{4,28},{6,30},{8,0},{10,2},{12,4},{14,6},{16,8},{18,... | collective-permute-start | bytes 835592 | tf_op jit(solution)/shard_map/ppermute | solution.py:441
  15.8 1.5 %collective-permute-start.6 = (bf16[136,1024]{1,0:T(8,128)(2,1)S(1)}, bf16[136,1024]{1,0:T(8,128)(2,1)S(1)}, u32[]{:S(2)}, u32[]{:S(2)}) collective-permute-start(bf16[136,1024]{1,0:T(8,128)(2,1)S(1)} %collective-permute-done.1.x0), channel_id=1, source_target_pairs={{0,4},{2,6},{4,0},{6,2},{8,12},{10,14},{12,8},{14,10},{16,20},{18,... | collective-permute-start | bytes 835592 | tf_op jit(solution)/shard_map/ppermute | solution.py:441
  17.3 0.0 collective-permute-done.4.x1
  17.3 1.7 %shard_map.103 = (bf16[8,256,1024]{2,1,0:T(8,128)(2,1)S(1)}, bf16[8,1024,256]{2,1,0:T(8,128)(2,1)S(1)}, bf16[2048,1024]{1,0:T(8,128)(2,1)S(1)}, bf16[16,8,256]{2,1,0:T(8,128)(2,1)S(1)}, f32[8,128]{1,0:T(8,128)S(1)}) custom-call(s32[1]{0:T(128)} %bitcast.here, ...), custom_call_target="tpu_custom_call", output_to_operand_aliasing={{0}: (6, {}), {1}: (7, {}), {2}: (8, {}), {3}: (9, {})} | custom-call | flops 1073741824 | bytes 6291456 | tf_op jit(solution)/shard_map/pallas_call | solution.py:187
  19.0 0.0 collective-permute-done.3.x1
  19.0 1.7 %shard_map.104 = (bf16[8,256,1024]{2,1,0:T(8,128)(2,1)S(1)}, bf16[8,1024,256]{2,1,0:T(8,128)(2,1)S(1)}, bf16[2048,1024]{1,0:T(8,128)(2,1)S(1)}, bf16[16,8,256]{2,1,0:T(8,128)(2,1)S(1)}, f32[8,128]{1,0:T(8,128)S(1)}) custom-call(s32[1]{0:T(128)} %bitcast.here, ...), custom_call_target="tpu_custom_call", output_to_operand_aliasing={{0}: (6, {}), {1}: (7, {}), {2}: (8, {}), {3}: (9, {})} | custom-call | flops 1073741824 | bytes 6291456 | tf_op jit(solution)/shard_map/pallas_call | solution.py:187
  20.7 1.8 %collective-permute-done.5.x0 = bf16[136,1024]{1,0:T(8,128)(2,1)S(1)} collective-permute-done((bf16[136,1024]{1,0:T(8,128)(2,1)S(1)}, bf16[136,1024]{1,0:T(8,128)(2,1)S(1)}, u32[]{:S(2)}, u32[]{:S(2)}) %collective-permute-start.5) | collective-permute-done | bytes 278560 | tf_op jit(solution)/shard_map/ppermute | solution.py:441
  22.6 0.0 collective-permute-start.8
  22.6 1.5 %collective-permute-done.6.x0 = bf16[136,1024]{1,0:T(8,128)(2,1)S(1)} collective-permute-done((bf16[136,1024]{1,0:T(8,128)(2,1)S(1)}, bf16[136,1024]{1,0:T(8,128)(2,1)S(1)}, u32[]{:S(2)}, u32[]{:S(2)}) %collective-permute-start.6) | collective-permute-done | bytes 278560 | tf_op jit(solution)/shard_map/ppermute | solution.py:441
  24.0 0.0 collective-permute-start.7
  24.1 0.3 collective-permute-start.9
  24.3 1.5 %collective-permute-start.10 = (bf16[136,1024]{1,0:T(8,128)(2,1)S(1)}, bf16[136,1024]{1,0:T(8,128)(2,1)S(1)}, u32[]{:S(2)}, u32[]{:S(2)}) collective-permute-start(bf16[136,1024]{1,0:T(8,128)(2,1)S(1)} %collective-permute-done.5.x0), channel_id=1, source_target_pairs={{0,4},{2,6},{4,0},{6,2},{8,12},{10,14},{12,8},{14,10},{16,20},{18,... | collective-permute-start | bytes 835592 | tf_op jit(solution)/shard_map/ppermute | solution.py:441
  25.9 0.0 collective-permute-done.8.x1
  25.9 1.7 %shard_map.105 = (bf16[8,256,1024]{2,1,0:T(8,128)(2,1)S(1)}, bf16[8,1024,256]{2,1,0:T(8,128)(2,1)S(1)}, bf16[2048,1024]{1,0:T(8,128)(2,1)S(1)}, bf16[16,8,256]{2,1,0:T(8,128)(2,1)S(1)}, f32[8,128]{1,0:T(8,128)S(1)}) custom-call(s32[1]{0:T(128)} %bitcast.here, ...), custom_call_target="tpu_custom_call", output_to_operand_aliasing={{0}: (6, {}), {1}: (7, {}), {2}: (8, {}), {3}: (9, {})} | custom-call | flops 1073741824 | bytes 6291456 | tf_op jit(solution)/shard_map/pallas_call | solution.py:187
  27.6 0.0 collective-permute-done.7.x1
  27.6 1.7 %shard_map.106 = (bf16[8,256,1024]{2,1,0:T(8,128)(2,1)S(1)}, bf16[8,1024,256]{2,1,0:T(8,128)(2,1)S(1)}, bf16[2048,1024]{1,0:T(8,128)(2,1)S(1)}, bf16[16,8,256]{2,1,0:T(8,128)(2,1)S(1)}, f32[8,128]{1,0:T(8,128)S(1)}) custom-call(s32[1]{0:T(128)} %bitcast.here, ...), custom_call_target="tpu_custom_call", output_to_operand_aliasing={{0}: (6, {}), {1}: (7, {}), {2}: (8, {}), {3}: (9, {})} | custom-call | flops 1073741824 | bytes 6291456 | tf_op jit(solution)/shard_map/pallas_call | solution.py:187
  29.3 5.6 %collective-permute-done.9.x0 = bf16[136,1024]{1,0:T(8,128)(2,1)S(1)} collective-permute-done((bf16[136,1024]{1,0:T(8,128)(2,1)S(1)}, bf16[136,1024]{1,0:T(8,128)(2,1)S(1)}, u32[]{:S(2)}, u32[]{:S(2)}) %collective-permute-start.9) | collective-permute-done | bytes 278560 | tf_op jit(solution)/shard_map/ppermute | solution.py:441
  34.9 0.0 collective-permute-start.12
  34.9 0.0 collective-permute-done.10.x0
  34.9 0.5 collective-permute-start.11
  35.4 0.0 collective-permute-start.13
  35.4 1.0 %collective-permute-done.12.x1 = bf16[136,1024]{1,0:T(8,128)(2,1)S(1)} collective-permute-done((bf16[136,1024]{1,0:T(8,128)(2,1)S(1)}, bf16[136,1024]{1,0:T(8,128)(2,1)S(1)}, u32[]{:S(2)}, u32[]{:S(2)}) %collective-permute-start.12) | collective-permute-done | bytes 278560 | tf_op jit(solution)/shard_map/ppermute | solution.py:441
  36.5 1.7 %shard_map.107 = (bf16[8,256,1024]{2,1,0:T(8,128)(2,1)S(1)}, bf16[8,1024,256]{2,1,0:T(8,128)(2,1)S(1)}, bf16[2048,1024]{1,0:T(8,128)(2,1)S(1)}, bf16[16,8,256]{2,1,0:T(8,128)(2,1)S(1)}, f32[8,128]{1,0:T(8,128)S(1)}) custom-call(s32[1]{0:T(128)} %bitcast.here, ...), custom_call_target="tpu_custom_call", output_to_operand_aliasing={{0}: (6, {}), {1}: (7, {}), {2}: (8, {}), {3}: (9, {})} | custom-call | flops 1073741824 | bytes 6291456 | tf_op jit(solution)/shard_map/pallas_call | solution.py:187
  38.2 0.0 collective-permute-done.11.x1
  38.2 1.7 %shard_map.108 = (bf16[8,256,1024]{2,1,0:T(8,128)(2,1)S(1)}, bf16[8,1024,256]{2,1,0:T(8,128)(2,1)S(1)}, bf16[2048,1024]{1,0:T(8,128)(2,1)S(1)}, bf16[16,8,256]{2,1,0:T(8,128)(2,1)S(1)}, f32[8,128]{1,0:T(8,128)S(1)}) custom-call(s32[1]{0:T(128)} %bitcast.here, ...), custom_call_target="tpu_custom_call", output_to_operand_aliasing={{0}: (6, {}), {1}: (7, {}), {2}: (8, {}), {3}: (9, {})} | custom-call | flops 1073741824 | bytes 6291456 | tf_op jit(solution)/shard_map/pallas_call | solution.py:187
  39.9 5.9 %collective-permute-done.13.x0 = bf16[136,1024]{1,0:T(8,128)(2,1)S(1)} collective-permute-done((bf16[136,1024]{1,0:T(8,128)(2,1)S(1)}, bf16[136,1024]{1,0:T(8,128)(2,1)S(1)}, u32[]{:S(2)}, u32[]{:S(2)}) %collective-permute-start.13) | collective-permute-done | bytes 278560 | tf_op jit(solution)/shard_map/ppermute | solution.py:441
  45.8 0.0 collective-permute-start.14
  45.8 1.6 %collective-permute-done.14.x1 = bf16[136,1024]{1,0:T(8,128)(2,1)S(1)} collective-permute-done((bf16[136,1024]{1,0:T(8,128)(2,1)S(1)}, bf16[136,1024]{1,0:T(8,128)(2,1)S(1)}, u32[]{:S(2)}, u32[]{:S(2)}) %collective-permute-start.14) | collective-permute-done | bytes 278560 | tf_op jit(solution)/shard_map/ppermute | solution.py:441
  47.4 0.0 copy-start.1
  47.4 0.0 copy-start.2
  47.4 2.2 %shard_map.109 = (bf16[8,256,1024]{2,1,0:T(8,128)(2,1)S(1)}, bf16[8,1024,256]{2,1,0:T(8,128)(2,1)S(1)}, bf16[2048,1024]{1,0:T(8,128)(2,1)S(1)}, bf16[16,8,256]{2,1,0:T(8,128)(2,1)S(1)}, f32[8,128]{1,0:T(8,128)}) custom-call(s32[1]{0:T(128)} %bitcast.here, ...), custom_call_target="tpu_custom_call", output_to_operand_aliasing={{0}: (6, {}), {1}: (7, {}), {2}: (8, {}), {3}: (9, {})} | custom-call | flops 1073741824 | bytes 6291456 | tf_op jit(solution)/shard_map/pallas_call | solution.py:187
  49.6 0.0 copy-done.1
  49.6 0.0 copy-done.2
  49.6 11.3 %shard_map.110 = bf16[768,512]{1,0:T(8,128)(2,1)} custom-call(s32[1]{0:T(128)} %bitcast.here, bf16[16,8,256]{2,1,0:T(8,128)(2,1)S(1)} %get-tuple-element.115.meta, f32[1,1024]{1,0:T(1,128)S(1)} %bitcast.14, f32[1,512]{1,0:T(1,128)S(1)} %bitcast.15, f32[1,512]{1,0:T(1,128)S(1)} %bitcast.16, bf16[2048,1024]{1,0:T(8,128)(2,1)S(1)} %get-tuple-element.116.xa, ...), custom_call_target="tpu_custom_call" | custom-call | tf_op jit(solution)/shard_map/pallas_call | solution.py:391
Async XLA Ops:
  0.0 8.6 %copy-start = (f32[1024]{0:T(1024)S(1)}, f32[1024]{0:T(1024)}, u32[]{:S(2)}) copy-start(f32[1024]{0:T(1024)} %param.13) | copy-start | bytes 12292
  1.0 7.6 %collective-permute-start = (bf16[136,1024]{1,0:T(8,128)(2,1)S(1)}, bf16[136,1024]{1,0:T(8,128)(2,1)S(1)}, u32[]{:S(2)}, u32[]{:S(2)}) collective-permute-start(bf16[136,1024]{1,0:T(8,128)(2,1)S(1)} %shard_map.100.x0), channel_id=1, source_target_pairs={{0,2},{2,0},{4,6},{6,4},{8,10},{10,8},{12,14},{14,12},{16,18},{18,... | collective-permute-start | bytes 835592 | tf_op jit(solution)/shard_map/ppermute | solution.py:441
  1.6 11.9 %collective-permute-start.1 = (bf16[136,1024]{1,0:T(8,128)(2,1)S(1)}, bf16[136,1024]{1,0:T(8,128)(2,1)S(1)}, u32[]{:S(2)}, u32[]{:S(2)}) collective-permute-start(bf16[136,1024]{1,0:T(8,128)(2,1)S(1)} %shard_map.100.x0), channel_id=1, source_target_pairs={{0,8},{2,10},{4,12},{6,14},{8,16},{10,18},{12,20},{14,22},{16,24},... | collective-permute-start | bytes 835592 | tf_op jit(solution)/shard_map/ppermute | solution.py:441
  4.2 9.3 %collective-permute-start.2 = (bf16[136,1024]{1,0:T(8,128)(2,1)S(1)}, bf16[136,1024]{1,0:T(8,128)(2,1)S(1)}, u32[]{:S(2)}, u32[]{:S(2)}) collective-permute-start(bf16[136,1024]{1,0:T(8,128)(2,1)S(1)} %shard_map.100.x0), channel_id=1, source_target_pairs={{0,4},{2,6},{4,0},{6,2},{8,12},{10,14},{12,8},{14,10},{16,20},{18,... | collective-permute-start | bytes 835592 | tf_op jit(solution)/shard_map/ppermute | solution.py:441
  13.5 3.8 %collective-permute-start.4 = (bf16[136,1024]{1,0:T(8,128)(2,1)S(1)}, bf16[136,1024]{1,0:T(8,128)(2,1)S(1)}, u32[]{:S(2)}, u32[]{:S(2)}) collective-permute-start(bf16[136,1024]{1,0:T(8,128)(2,1)S(1)} %collective-permute-done.1.x0), channel_id=1, source_target_pairs={{0,2},{2,0},{4,6},{6,4},{8,10},{10,8},{12,14},{14,12},{16,18},{18,... | collective-permute-start | bytes 835592 | tf_op jit(solution)/shard_map/ppermute | solution.py:441
  13.5 5.5 %collective-permute-start.3 = (bf16[136,1024]{1,0:T(8,128)(2,1)S(1)}, bf16[136,1024]{1,0:T(8,128)(2,1)S(1)}, u32[]{:S(2)}, u32[]{:S(2)}) collective-permute-start(bf16[136,1024]{1,0:T(8,128)(2,1)S(1)} %collective-permute-done.2.x0), channel_id=1, source_target_pairs={{0,2},{2,0},{4,6},{6,4},{8,10},{10,8},{12,14},{14,12},{16,18},{18,... | collective-permute-start | bytes 835592 | tf_op jit(solution)/shard_map/ppermute | solution.py:441
  14.0 8.6 %collective-permute-start.5 = (bf16[136,1024]{1,0:T(8,128)(2,1)S(1)}, bf16[136,1024]{1,0:T(8,128)(2,1)S(1)}, u32[]{:S(2)}, u32[]{:S(2)}) collective-permute-start(bf16[136,1024]{1,0:T(8,128)(2,1)S(1)} %shard_map.100.x0), channel_id=1, source_target_pairs={{0,24},{2,26},{4,28},{6,30},{8,0},{10,2},{12,4},{14,6},{16,8},{18,... | collective-permute-start | bytes 835592 | tf_op jit(solution)/shard_map/ppermute | solution.py:441
  15.8 8.3 %collective-permute-start.6 = (bf16[136,1024]{1,0:T(8,128)(2,1)S(1)}, bf16[136,1024]{1,0:T(8,128)(2,1)S(1)}, u32[]{:S(2)}, u32[]{:S(2)}) collective-permute-start(bf16[136,1024]{1,0:T(8,128)(2,1)S(1)} %collective-permute-done.1.x0), channel_id=1, source_target_pairs={{0,4},{2,6},{4,0},{6,2},{8,12},{10,14},{12,8},{14,10},{16,20},{18,... | collective-permute-start | bytes 835592 | tf_op jit(solution)/shard_map/ppermute | solution.py:441
  22.6 3.3 %collective-permute-start.8 = (bf16[136,1024]{1,0:T(8,128)(2,1)S(1)}, bf16[136,1024]{1,0:T(8,128)(2,1)S(1)}, u32[]{:S(2)}, u32[]{:S(2)}) collective-permute-start(bf16[136,1024]{1,0:T(8,128)(2,1)S(1)} %collective-permute-done.5.x0), channel_id=1, source_target_pairs={{0,2},{2,0},{4,6},{6,4},{8,10},{10,8},{12,14},{14,12},{16,18},{18,... | collective-permute-start | bytes 835592 | tf_op jit(solution)/shard_map/ppermute | solution.py:441
  24.0 3.5 %collective-permute-start.7 = (bf16[136,1024]{1,0:T(8,128)(2,1)S(1)}, bf16[136,1024]{1,0:T(8,128)(2,1)S(1)}, u32[]{:S(2)}, u32[]{:S(2)}) collective-permute-start(bf16[136,1024]{1,0:T(8,128)(2,1)S(1)} %collective-permute-done.6.x0), channel_id=1, source_target_pairs={{0,2},{2,0},{4,6},{6,4},{8,10},{10,8},{12,14},{14,12},{16,18},{18,... | collective-permute-start | bytes 835592 | tf_op jit(solution)/shard_map/ppermute | solution.py:441
  24.1 10.9 %collective-permute-start.9 = (bf16[136,1024]{1,0:T(8,128)(2,1)S(1)}, bf16[136,1024]{1,0:T(8,128)(2,1)S(1)}, u32[]{:S(2)}, u32[]{:S(2)}) collective-permute-start(bf16[136,1024]{1,0:T(8,128)(2,1)S(1)} %collective-permute-done.1.x0), channel_id=1, source_target_pairs={{0,8},{2,10},{4,12},{6,14},{8,16},{10,18},{12,20},{14,22},{16,24},... | collective-permute-start | bytes 835592 | tf_op jit(solution)/shard_map/ppermute | solution.py:441
  24.3 10.6 %collective-permute-start.10 = (bf16[136,1024]{1,0:T(8,128)(2,1)S(1)}, bf16[136,1024]{1,0:T(8,128)(2,1)S(1)}, u32[]{:S(2)}, u32[]{:S(2)}) collective-permute-start(bf16[136,1024]{1,0:T(8,128)(2,1)S(1)} %collective-permute-done.5.x0), channel_id=1, source_target_pairs={{0,4},{2,6},{4,0},{6,2},{8,12},{10,14},{12,8},{14,10},{16,20},{18,... | collective-permute-start | bytes 835592 | tf_op jit(solution)/shard_map/ppermute | solution.py:441
  34.9 1.6 %collective-permute-start.12 = (bf16[136,1024]{1,0:T(8,128)(2,1)S(1)}, bf16[136,1024]{1,0:T(8,128)(2,1)S(1)}, u32[]{:S(2)}, u32[]{:S(2)}) collective-permute-start(bf16[136,1024]{1,0:T(8,128)(2,1)S(1)} %collective-permute-done.9.x0), channel_id=1, source_target_pairs={{0,2},{2,0},{4,6},{6,4},{8,10},{10,8},{12,14},{14,12},{16,18},{18,... | collective-permute-start | bytes 835592 | tf_op jit(solution)/shard_map/ppermute | solution.py:441
  34.9 3.3 %collective-permute-start.11 = (bf16[136,1024]{1,0:T(8,128)(2,1)S(1)}, bf16[136,1024]{1,0:T(8,128)(2,1)S(1)}, u32[]{:S(2)}, u32[]{:S(2)}) collective-permute-start(bf16[136,1024]{1,0:T(8,128)(2,1)S(1)} %collective-permute-done.10.x0), channel_id=1, source_target_pairs={{0,2},{2,0},{4,6},{6,4},{8,10},{10,8},{12,14},{14,12},{16,18},{18,... | collective-permute-start | bytes 835592 | tf_op jit(solution)/shard_map/ppermute | solution.py:441
  35.4 10.4 %collective-permute-start.13 = (bf16[136,1024]{1,0:T(8,128)(2,1)S(1)}, bf16[136,1024]{1,0:T(8,128)(2,1)S(1)}, u32[]{:S(2)}, u32[]{:S(2)}) collective-permute-start(bf16[136,1024]{1,0:T(8,128)(2,1)S(1)} %collective-permute-done.6.x0), channel_id=1, source_target_pairs={{0,8},{2,10},{4,12},{6,14},{8,16},{10,18},{12,20},{14,22},{16,24},... | collective-permute-start | bytes 835592 | tf_op jit(solution)/shard_map/ppermute | solution.py:441
  45.8 1.6 %collective-permute-start.14 = (bf16[136,1024]{1,0:T(8,128)(2,1)S(1)}, bf16[136,1024]{1,0:T(8,128)(2,1)S(1)}, u32[]{:S(2)}, u32[]{:S(2)}) collective-permute-start(bf16[136,1024]{1,0:T(8,128)(2,1)S(1)} %collective-permute-done.13.x0), channel_id=1, source_target_pairs={{0,2},{2,0},{4,6},{6,4},{8,10},{10,8},{12,14},{14,12},{16,18},{18,... | collective-permute-start | bytes 835592 | tf_op jit(solution)/shard_map/ppermute | solution.py:441
  47.4 2.2 %copy-start.1 = (f32[512]{0:T(512)S(1)}, f32[512]{0:T(512)}, u32[]{:S(2)}) copy-start(f32[512]{0:T(512)} %param.18) | copy-start | bytes 6148
  47.4 2.2 %copy-start.2 = (f32[512]{0:T(512)S(1)}, f32[512]{0:T(512)}, u32[]{:S(2)}) copy-start(f32[512]{0:T(512)} %param.19) | copy-start | bytes 6148
